TPU v7x, 32 devices: a whole 2x2x4 slice. The times are simulated.
32 devices in a mesh: slab: 8 (over z, x), cross: 4 (over y, core).
Axes of the slice: x: 2, y: 2, z: 4, core: 2. Of those that a mesh axis runs over, the one named last changes fastest.
Arguments:
- les_state: float32 [54, 64, 16, 128], P(None, 'slab', 'cross'), may hold values from -6 to 6
- cmc_state: float32 [54, 128, 1024], P(None, 'cross', 'slab'), may hold values from -6 to 6
- cmc_map: int32 [64, 16, 128], P('slab', 'cross'), may hold values from 0 to 1023, as said below
- pdf_index: int32 [64, 16, 128], P('slab', 'cross'), may hold values from 0 to 127
- pdf_table: float32 [128, 128], replicated, may hold values from 0.001 to 0.05
- diffusion: float32 [54], replicated, may hold values from 0.02 to 0.15
- chem_matrix: float32 [54, 54], replicated, may hold values from -0.875 to 0.875
- dissipation: float32 [128, 1024], P('cross', 'slab'), may hold values from 0.05 to 0.2
- reaction_rate: float32 [128, 1024], P('cross', 'slab'), may hold values from 0.05 to 0.5
- substeps: int32 [1024], P('slab'), may hold values from 1 to 4
Outputs:
- les_out: float32 [54, 64, 16, 128], P(None, 'slab', 'cross')
- cmc_out: float32 [54, 128, 1024], P(None, 'cross', 'slab')
Inputs may be any that keep to these rules, and one draw needn't show every extreme that they name: `cmc_map`: an LES cell in plane x along the jet axis maps to a CMC cell whose index divided by 128 differs from x divided by 8 (both rounded down) by at most one.
All inputs are finite; a program needn't handle non-finite values.
Results may differ from a plain program's by a relative error of at most 0.0001.
Values sent between devices are 32-bit elements; how exact they have to be, the bound alone decides.
A program may use at most 128 MiB of HBM per device.

v0:
```python
import jax
import jax.numpy as jnp
from jax import lax
from jax.sharding import PartitionSpec as P

KMAX = 4


blend_weight = 1.0


def from_behind(array, axis, by):
    count = lax.axis_size(axis)
    pairs = [(i, i + by) for i in range(count) if 0 <= i + by < count]
    return lax.ppermute(array, axis, pairs)


def with_halo(cells, sides, width):
    for axis, dim in sides:
        count = lax.axis_size(axis)
        ends = count - 1
        head = lax.slice_in_dim(cells, 0, width, axis=dim)
        tail = lax.slice_in_dim(cells, cells.shape[dim] - width, cells.shape[dim], axis=dim)
        cells = jnp.concatenate(
            [
                lax.ppermute(tail, axis, [(i, (i + 1) % count) for i in range(ends)]),
                cells,
                lax.ppermute(head, axis, [((i + 1) % count, i) for i in range(ends)]),
            ],
            axis=dim,
        )
    return cells


def reduce_cross(numer, denom):
    return (
        lax.psum_scatter(numer, "cross", scatter_dimension=1, tiled=True),
        lax.psum_scatter(denom, "cross", scatter_dimension=1, tiled=True),
    )


def collect_blocks(numer, denom, cells):
    lower_n = numer[:, :, :cells]
    lower_d = denom[:, :, :cells]
    upper_n = numer[:, :, 2 * cells :]
    upper_d = denom[:, :, 2 * cells :]
    above_n, above_d = from_behind((lower_n, lower_d), "slab", -1)
    below_n, below_d = from_behind((upper_n, upper_d), "slab", 1)
    own_n = numer[:, :, cells : 2 * cells] + above_n + below_n
    own_d = denom[:, :, cells : 2 * cells] + above_d + below_d
    return (own_n, own_d)


def bin_sums(flat, keys, table, cells, nshape, species):
    highest = lax.Precision.HIGHEST
    grouped = jax.ops.segment_sum(flat.T, keys, num_segments=3 * cells * nshape).reshape(
        3 * cells, nshape, species
    )
    counted = jax.ops.segment_sum(
        jnp.ones(keys.shape, jnp.float32), keys, num_segments=3 * cells * nshape
    ).reshape(3 * cells, nshape)
    numer = jnp.einsum("mps,pb->sbm", grouped, table, precision=highest)
    denom = jnp.einsum("mp,pb->bm", counted, table, precision=highest)[None]
    return (numer, denom)


def bin_stencil(blended, banded, coeffs):
    return blended + coeffs[None] * (banded[:, 2:] - 2.0 * blended + banded[:, :-2])


def react(state, rates, counts, matrix):
    species = state.shape[0]
    for substep in range(KMAX):
        rate = jnp.dot(matrix, state.reshape(species, -1), precision=lax.Precision.HIGHEST).reshape(
            state.shape
        )
        active = (substep < counts)[None, None, :]
        state = jnp.where(active, state + 0.5 * rates[None] * jnp.tanh(rate), state)
    return state


def on_device(
    les_state,
    cmc_state,
    cmc_map,
    pdf_index,
    pdf_table,
    diffusion,
    chem_matrix,
    dissipation,
    reaction_rate,
    substeps,
):
    highest = lax.Precision.HIGHEST
    species = les_state.shape[0]
    cells = cmc_state.shape[2]
    nshape = pdf_table.shape[0]
    framed = with_halo(les_state, (("slab", 1), ("cross", 2)), 1)
    framed = jnp.pad(framed, ((0, 0), (0, 0), (0, 0), (1, 1)))
    neighbours = framed[:, 2:, 1:-1, 1:-1] + framed[:, :-2, 1:-1, 1:-1]
    neighbours = neighbours + framed[:, 1:-1, 2:, 1:-1] + framed[:, 1:-1, :-2, 1:-1]
    neighbours = neighbours + framed[:, 1:-1, 1:-1, 2:] + framed[:, 1:-1, 1:-1, :-2]
    transported = les_state + diffusion[:, None, None, None] * (neighbours - 6.0 * les_state)
    flat = transported.reshape(species, -1)
    shape_id = pdf_index.reshape(-1)
    offset = cmc_map.reshape(-1) - (lax.axis_index("slab") - 1) * cells
    keys = offset * nshape + shape_id
    numer, denom = bin_sums(flat, keys, pdf_table, cells, nshape, species)
    numer, denom = reduce_cross(numer, denom)
    numer, denom = collect_blocks(numer, denom, cells)
    edged = with_halo(cmc_state, (("slab", 2),), 1)
    left_cells = edged[:, :, :-2]
    right_cells = edged[:, :, 2:]
    moved = (
        cmc_state
        - 0.4 * (cmc_state - left_cells)
        + 0.1 * (right_cells - 2.0 * cmc_state + left_cells)
    )
    blended = (numer + blend_weight * moved) / (denom + blend_weight)
    banded = with_halo(blended, (("cross", 1),), 1)
    mixed = bin_stencil(blended, banded, dissipation)
    cmc_out = react(mixed, reaction_rate, substeps, chem_matrix)
    all_bins = lax.all_gather(cmc_out, "cross", axis=1, tiled=True)
    nearby = with_halo(all_bins, (("slab", 2),), cells)
    projected = jnp.einsum("pb,sbm->spm", pdf_table, nearby, precision=highest).reshape(species, -1)
    conditional = jnp.take(projected, shape_id * (3 * cells) + offset, axis=1)
    onehot = (shape_id[:, None] == jnp.arange(nshape, dtype=jnp.int32)[None, :]).astype(jnp.float32)
    cell_weight = jnp.dot(onehot, jnp.sum(pdf_table, axis=1), precision=highest)
    conditional = conditional / cell_weight[None, :]
    les_out = transported + 0.5 * (conditional.reshape(transported.shape) - transported)
    return (les_out, cmc_out)


def solution(mesh):
    return jax.shard_map(
        on_device,
        mesh=mesh,
        in_specs=(
            P(None, "slab", "cross", None),
            P(None, "cross", "slab"),
            P("slab", "cross", None),
            P("slab", "cross", None),
            P(),
            P(),
            P(),
            P("cross", "slab"),
            P("cross", "slab"),
            P("slab"),
        ),
        out_specs=(P(None, "slab", "cross", None), P(None, "cross", "slab")),
        check_vma=False,
    )
```

profile of v0, /device:TPU:0, one launch (start us, length us, event | category | flops | bytes accessed | tf_op | source)
XLA Modules:
  0.0 530.5 jit_solution(12718155009314643461)
XLA Ops:
  9.0 4.9 collective-permute-start.1
  17.9 2.6 collective-permute-done
  21.9 3.0 collective-permute-start.3
  28.1 2.1 copy.142
  30.2 32.5 %scatter_custom_fusion = f32[49152,54]{1,0:T(8,128)} fusion(s32[4096]{0:T(1024)S(1)} %bitcast.98, f32[4096,54]{1,0:T(8,128)} %copy.142, f32[]{:T(128)} %constant.19.clone.1), kind=kCustom, calls=%fused_computation.3 | custom fusion | flops 221184 | bytes 10617344 | tf_op jit(solution)/shard_map/scatter-add | solution.py:56
  62.7 19.2 %copy.143 = f32[384,128,54]{1,0,2:T(8,128)} copy(f32[384,128,54]{2,1,0:T(8,128)} %bitcast.73) | data formatting | bytes 21233664 | tf_op jit(solution)/shard_map/reshape | solution.py:56
  81.9 12.9 %convolution_bitcast_fusion = f32[54,128,384]{1,2,0:T(8,128)} fusion(f32[384,128,54]{1,0,2:T(8,128)} %copy.143, f32[128,128]{1,0:T(8,128)S(1)} %copy-done), kind=kOutput, calls=%fused_computation.18 | convolution fusion | flops 4076863488 | bytes 21299200 | tf_op jit(solution)/shard_map/mps,pb->sbm/dot_general | solution.py:62
  94.9 11.9 %copy.144 = f32[54,128,384]{2,0,1:T(8,128)} copy(f32[54,128,384]{1,2,0:T(8,128)} %convolution_bitcast_fusion) | data formatting | bytes 21233664 | tf_op jit(solution)/shard_map/mps,pb->sbm/transpose | solution.py:62
  106.9 21.9 %scatter_custom_fusion.1 = f32[49152]{0:T(1024)S(1)} fusion(s32[4096]{0:T(1024)S(1)} %bitcast.99, f32[4096]{0:T(1024)S(1)} %broadcast.87, f32[]{:T(128)} %constant.19.clone.1), kind=kCustom, calls=%fused_computation.67 | custom fusion | flops 4096 | bytes 196612 | tf_op jit(solution)/shard_map/scatter-add | solution.py:59
  128.8 71.3 %reduce-scatter.2.cloned.1.call-done = f32[54,32,384]{2,0,1:T(8,128)} async-done(((f32[54,128,384]{2,0,1:T(8,128)}), f32[54,32,384]{2,0,1:T(8,128)}) %reduce-scatter.2.cloned.1.call-update) | async-done | bytes 2654224 | tf_op jit(solution)/shard_map/reduce_scatter | solution.py:37
  200.1 1.9 fusion.43
  205.5 5.6 %collective-permute-start.5 = (f32[54,32,128]{2,1,0:T(8,128)}, f32[54,32,128]{2,1,0:T(8,128)}, u32[]{:S(2)}, u32[]{:S(2)}) collective-permute-start(f32[54,32,128]{2,1,0:T(8,128)} %copy.147), channel_id=1, source_target_pairs={{0,4},{4,8},{8,12},{12,16},{16,20},{20,24},{24,28},{1,5},{5,9},{9,... | collective-permute-start | bytes 2654216 | tf_op jit(solution)/shard_map/ppermute | solution.py:15
  215.6 3.3 collective-permute-start.6
  223.1 20.4 %all-reduce.4.cloned.1.call-done = f32[1,128,384]{2,0,1:T(1,128)} async-done(((f32[1,128,384]{2,0,1:T(1,128)}), f32[1,128,384]{2,0,1:T(1,128)}) %all-reduce.4.cloned.1.call-update) | async-done | bytes 196624
  246.0 4.4 collective-permute-start.9
  254.7 2.8 fusion.29
  258.8 3.3 collective-permute-start.11
  271.8 32.6 %all-gather.2.cloned.1.call-done = f32[54,128,128]{2,1,0:T(8,128)} async-done(((f32[54,32,128]{2,1,0:T(8,128)}), f32[54,128,128]{2,1,0:T(8,128)}) %all-gather.2.cloned.1.call-update) | async-done | bytes 3538960 | tf_op jit(solution)/shard_map/all_gather | solution.py:123
  304.3 5.2 copy.153
  309.5 5.2 collective-permute-start.12
  317.8 147.3 %collective-permute-done.12 = f32[54,128,128]{1,2,0:T(8,128)} collective-permute-done((f32[54,128,128]{1,2,0:T(8,128)}, f32[54,128,128]{1,2,0:T(8,128)}, u32[]{:S(2)}, u32[]{:S(2)}) %collective-permute-start.12) | collective-permute-done | bytes 3538976 | tf_op jit(solution)/shard_map/ppermute | solution.py:26
  465.2 12.8 %fusion.8 = f32[54,128,384]{1,2,0:T(8,128)} fusion(f32[54,128,128]{1,2,0:T(8,128)} %collective-permute-done.13, f32[54,128,128]{1,2,0:T(8,128)} %copy.153, f32[54,128,128]{1,2,0:T(8,128)} %collective-permute-done.12, f32[128,128]{1,0:T(8,128)S(1)} %copy-done), kind=kOutput, calls=%fused_computation.17 | convolution fusion | flops 4082171904 | bytes 21299200 | tf_op jit(solution)/shard_map/pb,sbm->spm/dot_general | solution.py:125
  478.0 22.9 %copy.162 = f32[54,128,384]{0,2,1:T(8,128)} copy(f32[54,128,384]{1,2,0:T(8,128)} %fusion.8) | data formatting | bytes 21233664 | tf_op jit(solution)/shard_map/reshape | solution.py:125
  500.9 18.9 %gather_fusion = f32[4096,54]{1,0:T(8,128)S(1)} fusion(f32[54,49152]{0,1:T(8,128)} %bitcast.74, s32[4096]{0:T(1024)S(1)} %broadcast_clamp_fusion), kind=kCustom, calls=%fused_computation | custom fusion | bytes 1785856 | tf_op jit(solution)/shard_map/jit(_take)/gather | solution.py:126
  (98 shorter events, 46.4 us)
Async XLA Ops:
  7.2 74.8 %copy-start = (f32[128,128]{1,0:T(8,128)S(1)}, f32[128,128]{1,0:T(8,128)}, u32[]{:S(2)}) copy-start(f32[128,128]{1,0:T(8,128)} %param.14) | copy-start | bytes 196612
  7.2 17.8 %copy-start.3 = (s32[8,4,128]{2,1,0:T(4,128)S(1)}, s32[8,4,128]{2,1,0:T(4,128)}, u32[]{:S(2)}) copy-start(s32[8,4,128]{2,1,0:T(4,128)} %param.13) | copy-start | bytes 49156
  7.2 192.9 %reduce-scatter.2.cloned.1.call-start = ((), (), s32[]{:S(2)}) async-start(), calls=%async_computation.1 | async-start | bytes 13762560 | tf_op jit(solution)/shard_map/reduce_scatter | solution.py:37
  9.0 7.3 %collective-permute-start.1 = (f32[54,1,4,128]{3,0,2,1:T(8,128)S(1)}, f32[54,1,4,128]{3,0,2,1:T(8,128)S(1)}, u32[]{:S(2)}, u32[]{:S(2)}) collective-permute-start(f32[54,1,4,128]{3,0,2,1:T(8,128)S(1)} %get-tuple-element.22), channel_id=1, source_target_pairs={{0,4},{4,8},{8,12},{12,16},{16,20},{20,24},{24,28},{1,5},{5,9},{9,... | collective-permute-start | bytes 331784 | tf_op jit(solution)/shard_map/ppermute | solution.py:26
  13.8 6.7 %collective-permute-start = (f32[54,1,4,128]{3,0,2,1:T(8,128)S(1)}, f32[54,1,4,128]{3,0,2,1:T(8,128)S(1)}, u32[]{:S(2)}, u32[]{:S(2)}) collective-permute-start(f32[54,1,4,128]{3,0,2,1:T(8,128)S(1)} %get-tuple-element.21), channel_id=1, source_target_pairs={{4,0},{8,4},{12,8},{16,12},{20,16},{24,20},{28,24},{5,1},{9,5},{13... | collective-permute-start | bytes 331784 | tf_op jit(solution)/shard_map/ppermute | solution.py:28
  20.6 4.4 collective-permute-start.2
  21.9 4.2 collective-permute-start.3
  106.8 136.8 %all-reduce.4.cloned.1.call-start = ((), (), s32[]{:S(2)}) async-start(), calls=%async_computation.3 | async-start | bytes 393216
  202.1 10.3 %copy-start.1 = (f32[54,32,128]{2,1,0:T(8,128)S(1)}, f32[54,32,128]{2,1,0:T(8,128)}, u32[]{:S(2)}) copy-start(f32[54,32,128]{2,1,0:T(8,128)} %param.11) | copy-start | bytes 2654212
  203.2 51.5 %collective-permute-start.4 = (f32[54,32,128]{2,1,0:T(8,128)}, f32[54,32,128]{2,1,0:T(8,128)}, u32[]{:S(2)}, u32[]{:S(2)}) collective-permute-start(f32[54,32,128]{2,1,0:T(8,128)} %copy.146), channel_id=1, source_target_pairs={{4,0},{8,4},{12,8},{16,12},{20,16},{24,20},{28,24},{5,1},{9,5},{13... | collective-permute-start | bytes 2654216 | tf_op jit(solution)/shard_map/ppermute | solution.py:15
  205.5 16.3 %copy-start.8 = (u32[32]{0:T(128)S(1)}, u32[32]{0:T(128)}, u32[]{:S(2)}) copy-start(u32[32]{0:T(128)} %constant.61) | copy-start | bytes 388
  205.5 44.9 %copy-start.5 = (f32[32,128]{1,0:T(8,128)S(1)}, f32[32,128]{1,0:T(8,128)}, u32[]{:S(2)}) copy-start(f32[32,128]{1,0:T(8,128)} %param.18) | copy-start | bytes 49156
  205.5 49.1 %collective-permute-start.5 = (f32[54,32,128]{2,1,0:T(8,128)}, f32[54,32,128]{2,1,0:T(8,128)}, u32[]{:S(2)}, u32[]{:S(2)}) collective-permute-start(f32[54,32,128]{2,1,0:T(8,128)} %copy.147), channel_id=1, source_target_pairs={{0,4},{4,8},{8,12},{12,16},{16,20},{20,24},{24,28},{1,5},{5,9},{9,... | collective-permute-start | bytes 2654216 | tf_op jit(solution)/shard_map/ppermute | solution.py:15
  212.3 92.0 %all-gather.2.cloned.1.call-start = ((), (), s32[]{:S(2)}) async-start(), calls=%async_computation.2 | async-start | bytes 4423680 | tf_op jit(solution)/shard_map/all_gather | solution.py:123
  215.6 30.5 %collective-permute-start.6 = (f32[54,32,1]{0,1,2:T(8,128)S(1)}, f32[54,32,1]{0,1,2:T(8,128)S(1)}, u32[]{:S(2)}, u32[]{:S(2)}) collective-permute-start(f32[54,32,1]{0,1,2:T(8,128)S(1)} %copy.165), channel_id=1, source_target_pairs={{0,4},{4,8},{8,12},{12,16},{16,20},{20,24},{24,28},{1,5},{5,9},{9,... | collective-permute-start | bytes 20744 | tf_op jit(solution)/shard_map/ppermute | solution.py:26
  220.6 31.6 %collective-permute-start.7 = (f32[54,32,1]{0,1,2:T(8,128)S(1)}, f32[54,32,1]{0,1,2:T(8,128)S(1)}, u32[]{:S(2)}, u32[]{:S(2)}) collective-permute-start(f32[54,32,1]{0,1,2:T(8,128)S(1)} %copy.166), channel_id=1, source_target_pairs={{4,0},{8,4},{12,8},{16,12},{20,16},{24,20},{28,24},{5,1},{9,5},{13... | collective-permute-start | bytes 20744 | tf_op jit(solution)/shard_map/ppermute | solution.py:28
  244.4 9.4 %collective-permute-start.8 = (f32[1,32,128]{2,0,1:T(1,128)S(1)}, f32[1,32,128]{2,0,1:T(1,128)S(1)}, u32[]{:S(2)}, u32[]{:S(2)}) collective-permute-start(f32[1,32,128]{2,0,1:T(1,128)S(1)} %get-tuple-element.27), channel_id=1, source_target_pairs={{4,0},{8,4},{12,8},{16,12},{20,16},{24,20},{28,24},{5,1},{9,5},{13... | collective-permute-start | bytes 49160 | tf_op jit(solution)/shard_map/ppermute | solution.py:15
  246.0 7.8 %collective-permute-start.9 = (f32[1,32,128]{2,0,1:T(1,128)S(1)}, f32[1,32,128]{2,0,1:T(1,128)S(1)}, u32[]{:S(2)}, u32[]{:S(2)}) collective-permute-start(f32[1,32,128]{2,0,1:T(1,128)S(1)} %get-tuple-element.28), channel_id=1, source_target_pairs={{0,4},{4,8},{8,12},{12,16},{16,20},{20,24},{24,28},{1,5},{5,9},{9,... | collective-permute-start | bytes 49160 | tf_op jit(solution)/shard_map/ppermute | solution.py:15
  252.1 10.0 %copy-start.7 = (s32[128]{0:T(128)S(1)}, s32[128]{0:T(128)}, u32[]{:S(2)}) copy-start(s32[128]{0:T(128)} %param.19) | copy-start | bytes 1540
  252.1 10.6 %copy-start.4 = (f32[32,128]{1,0:T(8,128)S(1)}, f32[32,128]{1,0:T(8,128)}, u32[]{:S(2)}) copy-start(f32[32,128]{1,0:T(8,128)} %param.17) | copy-start | bytes 49156
  257.5 4.6 collective-permute-start.10
  258.8 3.9 collective-permute-start.11
  309.5 155.7 %collective-permute-start.12 = (f32[54,128,128]{1,2,0:T(8,128)}, f32[54,128,128]{1,2,0:T(8,128)}, u32[]{:S(2)}, u32[]{:S(2)}) collective-permute-start(f32[54,128,128]{1,2,0:T(8,128)} %copy.153), channel_id=1, source_target_pairs={{0,4},{4,8},{8,12},{12,16},{16,20},{20,24},{24,28},{1,5},{5,9},{9,... | collective-permute-start | bytes 10616840 | tf_op jit(solution)/shard_map/ppermute | solution.py:26
  314.7 150.5 %collective-permute-start.13 = (f32[54,128,128]{1,2,0:T(8,128)}, f32[54,128,128]{1,2,0:T(8,128)}, u32[]{:S(2)}, u32[]{:S(2)}) collective-permute-start(f32[54,128,128]{1,2,0:T(8,128)} %copy.153), channel_id=1, source_target_pairs={{4,0},{8,4},{12,8},{16,12},{20,16},{24,20},{28,24},{5,1},{9,5},{13... | collective-permute-start | bytes 10616840 | tf_op jit(solution)/shard_map/ppermute | solution.py:28
  (2 other events, 15.3 us)
Sparse Core Ops, SparseCore 0:
  106.9 93.1 reduce-scatter.1
  212.5 31.0 all-reduce.3
  271.9 32.3 all-gather.1
where the time goes:
time: 533 us; the launch traced here: 530 us
  waiting for transfers between devices  277 us (52%)
  local copies, waits for them, and re-layouts  105 us (20%)
  other arithmetic  64 us (12%)
  starting transfers between devices  39.1 us (7%)
  matrix products  31.2 us (6%)
  between operations  14.9 us (3%)
    ppermute x5, waiting for transfers between devices, with_halo(): lax.ppermute(tail, axis, [(i, (i + 1) % count) for i in range(ends)])  150 us
    reduce_scatter x1, waiting for transfers between devices, reduce_cross(): lax.psum_scatter(numer, 'cross', scatter_dimension=1, tiled=True)  71.3 us
    all_gather x1, waiting for transfers between devices, on_device(): all_bins = lax.all_gather(cmc_out, 'cross', axis=1, tiled=True)  32.6 us
    scatter-add x1, other arithmetic, bin_sums(): jax.ops.segment_sum(flat.T, keys, num_segments=3 * cells * nshape)  32.5 us
    reshape x1, local copies, waits for them, and re-layouts, on_device(): jnp.einsum('pb,sbm->spm', pdf_table, nearby, precision=highest)  22.9 us
    scatter-add x1, other arithmetic, bin_sums(): jax.ops.segment_sum(jnp.ones(keys.shape, jnp.float32), keys, num_segments...  21.9 us
    gather x2, local copies, waits for them, and re-layouts, on_device(): conditional = jnp.take(projected, shape_id * (3 * cells) + offset, axis=1)  20.5 us
    unnamed x4, waiting for transfers between devices  20.5 us
  transfers between devices with their start and end apart: 17, of which 9 were waited for; matrix products, arithmetic and copies ran while one was open for 7% of the time, Pallas kernels for 0%

commit v1 on v0

v1 whole, which is shorter than its diff:
```python
import functools

import jax
import jax.numpy as jnp
from jax import lax
from jax.experimental import pallas as pl
from jax.experimental.pallas import tpu as pltpu
from jax.sharding import PartitionSpec as P

KMAX = 4
F32 = jnp.float32
BF16 = jnp.bfloat16
NT = (((1,), (1,)), ((), ()))
NN = (((1,), (0,)), ((), ()))


def shift(array, axis, by):
    count = lax.axis_size(axis)
    return lax.ppermute(array, axis, [(i, i + by) for i in range(count) if 0 <= i + by < count])


def swap(array, axis, bit):
    count = lax.axis_size(axis)
    return lax.ppermute(array, axis, [(i, i ^ bit) for i in range(count)])


def halves(x):
    high = x.astype(BF16)
    return high, (x - high.astype(F32)).astype(BF16)


def decode(row, nshape):
    cell = jnp.floor((row + 0.5) * (1.0 / nshape))
    return cell.astype(jnp.int32), (row - cell * nshape).astype(jnp.int32)


def rows_equal(targets, row):
    return jnp.where(targets == row, 1.0, 0.0).astype(BF16)


def bin_kernel(bins, sp, cells, nshape, outer, first, *refs):
    if outer:
        t_ref, w_ref, *refs = refs
        acc_ref = None if first else refs.pop(0)
        out_ref, wc_ref, lhs = refs
    else:
        t_ref, wc_ref, *refs = refs
        acc_ref = None if first else refs.pop(0)
        out_ref, lhs = refs
    ct = t_ref.shape[1]

    @pl.when(pl.program_id(0) == 0)
    def _():
        out_ref[...] = jnp.zeros_like(out_ref) if first else acc_ref[...]

    t = t_ref[...]
    cell, shape = decode(t[sp - 1 : sp, :], nshape)
    if outer:
        ids = lax.broadcasted_iota(jnp.int32, (nshape, ct), 0)
        table = w_ref[...]
        high, low = halves(table)
        rest = (table - high.astype(F32) - low.astype(F32)).astype(BF16)
        split = jnp.concatenate([high.astype(F32), low.astype(F32), rest.astype(F32)], axis=0).astype(BF16)
        parts = lax.dot_general(split, rows_equal(ids, shape), NN, preferred_element_type=F32)
        wb = table.shape[0]
        wc = parts[:wb] + parts[wb : 2 * wb] + parts[2 * wb :]
        wc_ref[...] = wc
        targets = lax.broadcasted_iota(jnp.int32, (2 * cells, ct), 0)
        targets = jnp.where(targets >= cells, targets + cells, targets)
    else:
        wc = wc_ref[...]
        targets = lax.broadcasted_iota(jnp.int32, (cells, ct), 0) + cells
    for b in range(0, bins, 2):
        prod = jnp.concatenate([t * wc[b : b + 1, :], t * wc[b + 1 : b + 2, :]], axis=0)
        high, low = halves(prod)
        lhs[b * sp : (b + 2) * sp, :ct] = high
        lhs[b * sp : (b + 2) * sp, ct:] = low
    hot = rows_equal(targets, cell)
    hot = jnp.concatenate([hot, hot], axis=1)
    out_ref[...] += lax.dot_general(lhs[...], hot, NT, preferred_element_type=F32)


def bin_call(t, w, wc, acc, bins, cells, nshape, ct=512):
    sp, count = t.shape
    outer = wc is None
    width = (2 if outer else 1) * cells
    rows = bins * sp
    whole = lambda shape: pl.BlockSpec(shape, lambda i: (0,) * len(shape))
    col = lambda r: pl.BlockSpec((r, ct), lambda i: (0, i))
    wb = w.shape[0]
    args, specs = [t], [col(sp)]
    if outer:
        args.append(w)
        specs.append(whole(w.shape))
    else:
        args.append(wc)
        specs.append(col(wb))
    if acc is not None:
        args.append(acc)
        specs.append(whole(acc.shape))
    shapes = [jax.ShapeDtypeStruct((rows, width), F32)]
    outs = [whole((rows, width))]
    if outer:
        shapes.append(jax.ShapeDtypeStruct((wb, count), F32))
        outs.append(col(wb))
    flops = 4 * rows * width * count
    res = pl.pallas_call(
        functools.partial(bin_kernel, bins, sp, cells, nshape, outer, acc is None),
        grid=(count // ct,),
        out_shape=shapes,
        in_specs=specs,
        out_specs=outs,
        scratch_shapes=[pltpu.VMEM((rows, 2 * ct), BF16)],
        compiler_params=pltpu.CompilerParams(vmem_limit_bytes=40 << 20),
        cost_estimate=pl.CostEstimate(flops=flops, bytes_accessed=4 * sp * count, transcendentals=0),
        name="bin_outer" if outer else "bin_own",
    )(*args)
    return res if outer else res[0]


def chem_kernel(species, sp, own_ref, above_ref, below_ref, moved_ref, diss_ref, rate_ref, count_ref, matrix_ref, out_ref):
    bins = out_ref.shape[0]
    matrix = matrix_ref[...]
    count = count_ref[...]
    row = lax.broadcasted_iota(jnp.int32, (sp, out_ref.shape[2]), 0)

    def blend(b):
        total = own_ref[b] + above_ref[b] + below_ref[b]
        return (total + moved_ref[b]) / (total[species : species + 1, :] + 1.0)

    before, here = blend(0), blend(1)
    for b in range(bins):
        after = blend(b + 2)
        state = here + diss_ref[b : b + 1, :] * (after - 2.0 * here + before)
        half = 0.5 * rate_ref[b : b + 1, :]
        for k in range(KMAX):
            rate = lax.dot_general(matrix, state, NN, precision=lax.Precision.HIGHEST, preferred_element_type=F32)
            state = jnp.where(k < count, state + half * jnp.tanh(rate), state)
        out_ref[b] = jnp.where(row == species, 1.0, state)
        before, here = here, after


def project_kernel(bins, sp, cells, nshape, groups, accumulate, *refs):
    xs, refs = refs[: len(groups)], refs[len(groups) :]
    key_ref, wc_ref, *refs = refs
    acc_ref = refs.pop(0) if accumulate else None
    out_ref, lhs = refs
    ct = out_ref.shape[1]

    @pl.when(pl.program_id(0) == 0)
    def _():
        for n, x_ref in enumerate(xs):
            high, low = halves(x_ref[...])
            lhs[:, 2 * n * cells : (2 * n + 1) * cells] = high
            lhs[:, (2 * n + 1) * cells : (2 * n + 2) * cells] = low

    cell, _ = decode(key_ref[7:8, :], nshape)
    ids = lax.broadcasted_iota(jnp.int32, (cells, ct), 0)
    hots = []
    for g in groups:
        hot = rows_equal(ids + g * cells, cell)
        hots += [hot, hot]
    y = lax.dot_general(lhs[...], jnp.concatenate(hots, axis=0), NN, preferred_element_type=F32)
    total = acc_ref[...] if accumulate else jnp.zeros((sp, ct), F32)
    for b in range(bins):
        total = total + wc_ref[b + 1 : b + 2, :] * y[b * sp : (b + 1) * sp]
    out_ref[...] = total


def project_call(xs, groups, t, wc, acc, bins, cells, nshape, ct=256):
    sp, count = t.shape
    rows = bins * sp
    whole = lambda shape: pl.BlockSpec(shape, lambda i: (0,) * len(shape))
    col = lambda r: pl.BlockSpec((r, ct), lambda i: (0, i))
    args = list(xs) + [t, wc]
    specs = [whole(x.shape) for x in xs] + [pl.BlockSpec((8, ct), lambda i: (sp // 8 - 1, i)), col(wc.shape[0])]
    if acc is not None:
        args.append(acc)
        specs.append(col(sp))
    return pl.pallas_call(
        functools.partial(project_kernel, bins, sp, cells, nshape, groups, acc is not None),
        grid=(count // ct,),
        out_shape=jax.ShapeDtypeStruct((sp, count), F32),
        in_specs=specs,
        out_specs=col(sp),
        scratch_shapes=[pltpu.VMEM((rows, 2 * len(groups) * cells), BF16)],
        compiler_params=pltpu.CompilerParams(vmem_limit_bytes=40 << 20),
        cost_estimate=pl.CostEstimate(flops=4 * rows * cells * len(groups) * count, bytes_accessed=8 * sp * count, transcendentals=0),
        name="project",
    )(*args)


def on_device(
    les_state, cmc_state, cmc_map, pdf_index, pdf_table, diffusion, chem_matrix, dissipation, reaction_rate, substeps
):
    species = les_state.shape[0]
    sp = -(-(species + 2) // 8) * 8
    own_bins, cells = cmc_state.shape[1:]
    bins = own_bins + 2
    nshape = pdf_table.shape[0]
    count = cmc_map.size
    ncross = lax.axis_size("cross")

    below = shift(les_state[:, -1:], "slab", 1)
    above = shift(les_state[:, :1], "slab", -1)
    behind = shift(les_state[:, :, -1:], "cross", 1)
    ahead = shift(les_state[:, :, :1], "cross", -1)
    xs = jnp.concatenate([below, les_state, above], axis=1)
    ys = jnp.concatenate([behind, les_state, ahead], axis=2)
    zs = jnp.pad(les_state, ((0, 0), (0, 0), (0, 0), (1, 1)))
    around = xs[:, 2:] + xs[:, :-2] + ys[:, :, 2:] + ys[:, :, :-2] + zs[..., 2:] + zs[..., :-2]
    transported = les_state + diffusion[:, None, None, None] * (around - 6.0 * les_state)
    flat = transported.reshape(species, count)
    offset = cmc_map.reshape(1, count) - (lax.axis_index("slab") - 1) * cells
    key = (offset * nshape + pdf_index.reshape(1, count)).astype(F32)
    rows = [flat] + [jnp.ones((1, count), F32)] + [jnp.zeros((sp - species - 2, count), F32)] * (sp > species + 2) + [key]
    t_own = jnp.concatenate(rows, axis=0)

    wb = -(-bins // 8) * 8
    table = jnp.pad(pdf_table.T, ((1, wb - own_bins - 1), (0, 0)))
    table = lax.dynamic_slice_in_dim(table, lax.axis_index("cross") * own_bins, wb, axis=0)
    used = lax.broadcasted_iota(jnp.int32, (wb, 1), 0) < bins
    table = jnp.where(used, table, 0.0)

    blocks = [t_own]
    bits = [1 << k for k in range(ncross.bit_length() - 1)][::-1]
    for bit in bits:
        blocks.append(swap(jnp.concatenate(blocks, axis=1) if len(blocks) > 1 else blocks[0], "cross", bit))

    acc, wcs = None, []
    for block in blocks:
        acc, wc = bin_call(block, table, None, acc, bins, cells, nshape)
        wcs.append(wc)
    up = shift(acc[:, cells:], "slab", 1)
    down = shift(acc[:, :cells], "slab", -1)
    mine = None
    for block, wc in zip(blocks, wcs):
        mine = bin_call(block, table, wc, mine, bins, cells, nshape)

    left_cells = jnp.concatenate([shift(cmc_state[:, :, -1:], "slab", 1), cmc_state[:, :, :-1]], axis=2)
    right_cells = jnp.concatenate([cmc_state[:, :, 1:], shift(cmc_state[:, :, :1], "slab", -1)], axis=2)
    moved = cmc_state - 0.4 * (cmc_state - left_cells) + 0.1 * (right_cells - 2.0 * cmc_state + left_cells)
    moved = jnp.concatenate(
        [shift(moved[:, -1:], "cross", 1), moved, shift(moved[:, :1], "cross", -1)], axis=1
    )
    moved = jnp.pad(moved.transpose(1, 0, 2), ((0, 0), (0, sp - species), (0, 0)))

    cube = lambda a: a.reshape(bins, sp, cells)
    extra = sp - species
    fresh = pl.pallas_call(
        functools.partial(chem_kernel, species, sp),
        out_shape=jax.ShapeDtypeStruct((own_bins, sp, cells), F32),
        compiler_params=pltpu.CompilerParams(vmem_limit_bytes=40 << 20),
        name="chem",
    )(
        cube(mine), cube(up), cube(down), moved, dissipation, reaction_rate, substeps[None, :],
        jnp.pad(chem_matrix, ((0, extra), (0, extra))),
    )
    cmc_out = fresh[:, :species].transpose(1, 0, 2)
    fresh = fresh.reshape(own_bins * sp, cells)
    from_below = shift(fresh, "slab", 1)
    from_above = shift(fresh, "slab", -1)

    args = (own_bins, cells, nshape)
    own_part = [project_call([fresh], (1,), b, w, None, *args) for b, w in zip(blocks, wcs)]
    parts = [None] * len(blocks)
    for n in reversed(range(len(blocks))):
        parts[n] = project_call([from_below, from_above], (0, 2), blocks[n], wcs[n], own_part[n], *args)
    for n, bit in reversed(list(enumerate(bits))):
        got = swap(parts[n + 1], "cross", bit)
        parts[0 : n + 1] = [
            p + got[:, sum(q.shape[1] for q in parts[:k]) :][:, : p.shape[1]] for k, p in enumerate(parts[: n + 1])
        ]
    total = parts[0]
    conditional = (total[:species] / total[species : species + 1]).reshape(transported.shape)
    les_out = transported + 0.5 * (conditional - transported)
    return (les_out, cmc_out)


def solution(mesh):
    return jax.shard_map(
        on_device,
        mesh=mesh,
        in_specs=(
            P(None, "slab", "cross", None),
            P(None, "cross", "slab"),
            P("slab", "cross", None),
            P("slab", "cross", None),
            P(),
            P(),
            P(),
            P("cross", "slab"),
            P("cross", "slab"),
            P("slab"),
        ),
        out_specs=(P(None, "slab", "cross", None), P(None, "cross", "slab")),
        check_vma=False,
    )
```

time: 533 us -> 291 us (0.55)
  waiting for transfers between devices: 277 us -> 42.3 us
  Pallas kernels: 0 us -> 179 us
  local copies, waits for them, and re-layouts: 105 us -> 21.9 us
  other arithmetic: 64 us -> 8.58 us
  matrix products: 31.2 us -> 0 us
  between operations: 14.9 us -> 1.08 us
    pallas_call x0 -> x13, Pallas kernels: none -> 179 us  [the longest x6 86.2 us: bin_call(): pl.pallas_call(functools.partial(bin_kernel, bins, sp, cells, nshape, out...]
    ppermute x14 -> x16, waiting for transfers between devices: 152 us -> 42.3 us  [the longest x12 34.9 us: shift(): lax.ppermute(array, axis, [(i, i + by) for i in range(count) if 0 <= i +...]
    reduce_scatter x1 -> x0, waiting for transfers between devices: 71.3 us -> none  [reduce_cross(): lax.psum_scatter(numer, 'cross', scatter_dimension=1, tiled=True)]
    scatter-add x2 -> x0, other arithmetic: 54.5 us -> none  [the longest x1 32.5 us: bin_sums(): jax.ops.segment_sum(flat.T, keys, num_segments=3 * cells * nshape)]
    reshape x3 -> x2, local copies, waits for them, and re-layouts: 42.5 us -> 2.15 us  [the longest x1 1.55 us: on_device(): flat = transported.reshape(species, count)]
    all_gather x1 -> x0, waiting for transfers between devices: 32.6 us -> none  [on_device(): all_bins = lax.all_gather(cmc_out, 'cross', axis=1, tiled=True)]
    dot_general x8 -> x0, matrix products: 31.2 us -> none  [the longest x1 12.9 us: bin_sums(): numer = jnp.einsum('mps,pb->sbm', grouped, table, precision=highest)]
    gather x2 -> x0, local copies, waits for them, and re-layouts: 20.5 us -> none  [on_device(): conditional = jnp.take(projected, shape_id * (3 * cells) + offset, axis=1)]
  transfers between devices with their start and end apart: 17 -> 16, of which waited for: 9 -> 6; matrix products, arithmetic and copies ran while one was open for 7% -> 8% of each run, Pallas kernels for 0% -> 40%
where the time goes in v1:
time: 291 us; the launch traced here: 290 us
  Pallas kernels  179 us (62%)
  waiting for transfers between devices  42.3 us (15%)
  starting transfers between devices  37.6 us (13%)
  local copies, waits for them, and re-layouts  21.9 us (8%)
  other arithmetic  8.58 us (3%)
    pallas_call x6, Pallas kernels, bin_call(): pl.pallas_call(functools.partial(bin_kernel, bins, sp, cells, nshape, out...  86.2 us
    pallas_call x6, Pallas kernels, project_call(): pl.pallas_call(functools.partial(project_kernel, bins, sp, cells, nshape,...  75.8 us
    ppermute x12, waiting for transfers between devices, shift(): lax.ppermute(array, axis, [(i, i + by) for i in range(count) if 0 <= i +...  34.9 us
    ppermute x12, starting transfers between devices, shift(): lax.ppermute(array, axis, [(i, i + by) for i in range(count) if 0 <= i +...  31.9 us
    pallas_call x1, Pallas kernels, on_device(): pl.pallas_call(functools.partial(chem_kernel, species, sp), out_shape=jax...  16.7 us
    unnamed x34, local copies, waits for them, and re-layouts  9.13 us
    ppermute x4, waiting for transfers between devices, swap(): return lax.ppermute(array, axis, [(i, i ^ bit) for i in range(count)])  7.37 us
  transfers between devices with their start and end apart: 16, of which 6 were waited for; matrix products, arithmetic and copies ran while one was open for 8% of the time, Pallas kernels for 40%

profile of v1, /device:TPU:0, one launch (start us, length us, event | category | flops | bytes accessed | tf_op | source)
XLA Modules:
  0.0 290.1 jit_solution(6064814902289645782)
XLA Ops:
  3.6 5.5 %collective-permute-start.1 = (f32[54,1,4,128]{3,2,1,0:T(4,128)}, f32[54,1,4,128]{3,2,1,0:T(4,128)S(1)}, u32[]{:S(2)}, u32[]{:S(2)}) collective-permute-start(f32[54,1,4,128]{3,2,1,0:T(4,128)} %get-tuple-element.27), channel_id=1, source_target_pairs={{0,4},{4,8},{8,12},{12,16},{16,20},{20,24},{24,28},{1,5},{5,9},{9,... | collective-permute-start | bytes 331784 | tf_op jit(solution)/shard_map/ppermute | solution.py:19
  20.3 5.9 %collective-permute-start.8 = (f32[54,32,1]{0,1,2:T(8,128)}, f32[54,32,1]{0,1,2:T(8,128)}, u32[]{:S(2)}, u32[]{:S(2)}) collective-permute-start(f32[54,32,1]{0,1,2:T(8,128)} %copy.38), channel_id=1, source_target_pairs={{0,4},{4,8},{8,12},{12,16},{16,20},{20,24},{24,28},{1,5},{5,9},{9,... | collective-permute-start | bytes 20744 | tf_op jit(solution)/shard_map/ppermute | solution.py:19
  31.1 4.6 %collective-permute-start.4 = (f32[56,4096]{1,0:T(8,128)S(1)}, f32[56,4096]{1,0:T(8,128)S(1)}, u32[]{:S(2)}, u32[]{:S(2)}) collective-permute-start(f32[56,4096]{1,0:T(8,128)S(1)} %pad_maximum_fusion.1.refs_0_.refs_1_.refs_2_), channel_id=1, source_target_pairs={{0,2},{1,3},{2,0},{3,1},{4,6},{5,7},{6,4},{7,5},{8,10},{9,11},{10,... | collective-permute-start | bytes 2752520 | tf_op jit(solution)/shard_map/ppermute | solution.py:24
  44.1 2.9 fusion.3
  51.8 4.3 %collective-permute-done.4.refs_0_.refs_1_.refs_2_ = f32[56,4096]{1,0:T(8,128)S(1)} collective-permute-done((f32[56,4096]{1,0:T(8,128)S(1)}, f32[56,4096]{1,0:T(8,128)S(1)}, u32[]{:S(2)}, u32[]{:S(2)}) %collective-permute-start.4) | collective-permute-done | bytes 917536 | tf_op jit(solution)/shard_map/ppermute | solution.py:24
  56.6 11.4 %bin_outer.3 = (f32[1904,256]{1,0:T(8,128)S(1)}, f32[40,4096]{1,0:T(8,128)S(1)}) custom-call(f32[56,4096]{1,0:T(8,128)S(1)} %pad_maximum_fusion.1.refs_0_.refs_1_.refs_2_, f32[40,128]{1,0:T(8,128)S(1)} %fusion.12.refs_1_), custom_call_target="tpu_custom_call" | custom-call | flops 7985954816 | bytes 917504 | tf_op jit(solution)/shard_map/bin_outer/pallas_call | solution.py:107
  68.0 10.2 %bin_own.3.refs_2_ = f32[1904,128]{1,0:T(8,128)S(1)} custom-call(f32[56,4096]{1,0:T(8,128)S(1)} %pad_maximum_fusion.1.refs_0_.refs_1_.refs_2_, f32[40,4096]{1,0:T(8,128)S(1)} %get-tuple-element.12.refs_1_.refs_2_.refs_3_), custom_call_target="tpu_custom_call" | custom-call | flops 3992977408 | bytes 917504 | tf_op jit(solution)/shard_map/bin_own/pallas_call | solution.py:107
  78.2 11.4 %bin_outer.4 = (f32[1904,256]{1,0:T(8,128)S(1)}, f32[40,4096]{1,0:T(8,128)S(1)}) custom-call(f32[56,4096]{1,0:T(8,128)S(1)} %collective-permute-done.4.refs_0_.refs_1_.refs_2_, f32[40,128]{1,0:T(8,128)S(1)} %fusion.12.refs_1_, f32[1904,256]{1,0:T(8,128)S(1)} %get-tuple-element.8.refs_2_), custom_call_target="tpu_custom_call" | custom-call | flops 7985954816 | bytes 917504 | tf_op jit(solution)/shard_map/bin_outer/pallas_call | solution.py:107
  89.7 22.7 %bin_outer.5 = (f32[1904,256]{1,0:T(8,128)S(1)}, f32[40,8192]{1,0:T(8,128)S(1)}) custom-call(f32[56,8192]{1,0:T(8,128)S(1)} %collective-permute-done.5.refs_0_.refs_1_.refs_2_, f32[40,128]{1,0:T(8,128)S(1)} %fusion.12.refs_1_, f32[1904,256]{1,0:T(8,128)S(1)} %get-tuple-element.9.refs_2_), custom_call_target="tpu_custom_call" | custom-call | flops 15971909632 | bytes 1835008 | tf_op jit(solution)/shard_map/bin_outer/pallas_call | solution.py:107
  113.8 4.6 %collective-permute-start.6 = (f32[1904,128]{1,0:T(8,128)S(1)}, f32[1904,128]{1,0:T(8,128)S(1)}, u32[]{:S(2)}, u32[]{:S(2)}) collective-permute-start(f32[1904,128]{1,0:T(8,128)S(1)} %get-tuple-element.19), channel_id=1, source_target_pairs={{0,4},{4,8},{8,12},{12,16},{16,20},{20,24},{24,28},{1,5},{5,9},{9,... | collective-permute-start | bytes 2924552 | tf_op jit(solution)/shard_map/ppermute | solution.py:19
  118.4 9.9 %bin_own.4.refs_2_ = f32[1904,128]{1,0:T(8,128)S(1)} custom-call(f32[56,4096]{1,0:T(8,128)S(1)} %collective-permute-done.4.refs_0_.refs_1_.refs_2_, f32[40,4096]{1,0:T(8,128)S(1)} %get-tuple-element.11.refs_1_.refs_2_.refs_3_, f32[1904,128]{1,0:T(8,128)S(1)} %bin_own.3.refs_2_), custom_call_target="tpu_custom_call" | custom-call | flops 3992977408 | bytes 917504 | tf_op jit(solution)/shard_map/bin_own/pallas_call | solution.py:107
  128.4 20.6 %bin_own.5 = f32[1904,128]{1,0:T(8,128)S(1)} custom-call(f32[56,8192]{1,0:T(8,128)S(1)} %collective-permute-done.5.refs_0_.refs_1_.refs_2_, f32[40,8192]{1,0:T(8,128)S(1)} %get-tuple-element.10.refs_1_.refs_2_.refs_3_, f32[1904,128]{1,0:T(8,128)S(1)} %bin_own.4.refs_2_), custom_call_target="tpu_custom_call" | custom-call | flops 7985954816 | bytes 1835008 | tf_op jit(solution)/shard_map/bin_own/pallas_call | solution.py:107
  149.0 10.5 %collective-permute-done.6 = f32[1904,128]{1,0:T(8,128)S(1)} collective-permute-done((f32[1904,128]{1,0:T(8,128)S(1)}, f32[1904,128]{1,0:T(8,128)S(1)}, u32[]{:S(2)}, u32[]{:S(2)}) %collective-permute-start.6) | collective-permute-done | bytes 974880 | tf_op jit(solution)/shard_map/ppermute | solution.py:19
  159.5 16.7 %chem.1 = f32[32,56,128]{2,1,0:T(8,128)S(1)} custom-call(f32[34,56,128]{2,1,0:T(8,128)S(1)} %bitcast.23, f32[34,56,128]{2,1,0:T(8,128)S(1)} %bitcast.22, f32[34,56,128]{2,1,0:T(8,128)S(1)} %bitcast.21, f32[34,56,128]{2,1,0:T(8,128)S(1)} %pad.18.moved_ref, f32[32,128]{1,0:T(8,128)S(1)} %copy-done, f32[32,128]{1,0:T(8,128)S(1)} %copy-done.1, ...), custom_call_target="tpu_custom_call" | custom-call | tf_op jit(solution)/shard_map/chem/pallas_call | solution.py:250
  177.5 5.1 %collective-permute-start.12 = (f32[1792,128]{1,0:T(8,128)S(1)}, f32[1792,128]{1,0:T(8,128)S(1)}, u32[]{:S(2)}, u32[]{:S(2)}) collective-permute-start(f32[1792,128]{1,0:T(8,128)S(1)} %bitcast.17), channel_id=1, source_target_pairs={{0,4},{4,8},{8,12},{12,16},{16,20},{20,24},{24,28},{1,5},{5,9},{9,... | collective-permute-start | bytes 2752520 | tf_op jit(solution)/shard_map/ppermute | solution.py:19
  182.6 15.7 %project.8.refs_4_ = f32[56,8192]{1,0:T(8,128)S(1)} custom-call(f32[1792,128]{1,0:T(8,128)S(1)} %bitcast.18, f32[56,8192]{1,0:T(8,128)S(1)} %collective-permute-done.5.refs_0_.refs_1_.refs_2_, f32[40,8192]{1,0:T(8,128)S(1)} %get-tuple-element.10.refs_1_.refs_2_.refs_3_), custom_call_target="tpu_custom_call" | custom-call | flops 7516192768 | bytes 3670016 | tf_op jit(solution)/shard_map/project/pallas_call | solution.py:180
  198.2 2.9 collective-permute-done.13.refs_1_
  201.1 19.8 %collective-permute-done.12.refs_0_ = f32[1792,128]{1,0:T(8,128)S(1)} collective-permute-done((f32[1792,128]{1,0:T(8,128)S(1)}, f32[1792,128]{1,0:T(8,128)S(1)}, u32[]{:S(2)}, u32[]{:S(2)}) %collective-permute-start.12) | collective-permute-done | bytes 917536 | tf_op jit(solution)/shard_map/ppermute | solution.py:19
  220.9 22.0 %project.9 = f32[56,8192]{1,0:T(8,128)S(1)} custom-call(f32[1792,128]{1,0:T(8,128)S(1)} %collective-permute-done.12.refs_0_, f32[1792,128]{1,0:T(8,128)S(1)} %collective-permute-done.13.refs_1_, f32[56,8192]{1,0:T(8,128)S(1)} %collective-permute-done.5.refs_0_.refs_1_.refs_2_, f32[40,8192]{1,0:T(8,128)S(1)} %get-tuple-element.10.refs_1_.refs_2_.refs_3_, ...), custom_call_target="tpu_custom_call" | custom-call | flops 15032385536 | bytes 3670016 | tf_op jit(solution)/shard_map/project/pallas_call | solution.py:180
  244.2 7.8 %project.10.refs_4_ = f32[56,4096]{1,0:T(8,128)S(1)} custom-call(f32[1792,128]{1,0:T(8,128)S(1)} %bitcast.19, f32[56,4096]{1,0:T(8,128)S(1)} %collective-permute-done.4.refs_0_.refs_1_.refs_2_, f32[40,4096]{1,0:T(8,128)S(1)} %get-tuple-element.11.refs_1_.refs_2_.refs_3_), custom_call_target="tpu_custom_call" | custom-call | flops 3758096384 | bytes 1835008 | tf_op jit(solution)/shard_map/project/pallas_call | solution.py:180
  252.0 11.2 %project.11 = f32[56,4096]{1,0:T(8,128)S(1)} custom-call(f32[1792,128]{1,0:T(8,128)S(1)} %collective-permute-done.12.refs_0_, f32[1792,128]{1,0:T(8,128)S(1)} %collective-permute-done.13.refs_1_, f32[56,4096]{1,0:T(8,128)S(1)} %collective-permute-done.4.refs_0_.refs_1_.refs_2_, f32[40,4096]{1,0:T(8,128)S(1)} %get-tuple-element.11.refs_1_.refs_2_.refs_3_, ...), custom_call_target="tpu_custom_call" | custom-call | flops 7516192768 | bytes 1835008 | tf_op jit(solution)/shard_map/project/pallas_call | solution.py:180
  264.1 7.8 %project.6.refs_4_ = f32[56,4096]{1,0:T(8,128)S(1)} custom-call(f32[1792,128]{1,0:T(8,128)S(1)} %bitcast.20, f32[56,4096]{1,0:T(8,128)S(1)} %pad_maximum_fusion.1.refs_0_.refs_1_.refs_2_, f32[40,4096]{1,0:T(8,128)S(1)} %get-tuple-element.12.refs_1_.refs_2_.refs_3_), custom_call_target="tpu_custom_call" | custom-call | flops 3758096384 | bytes 1835008 | tf_op jit(solution)/shard_map/project/pallas_call | solution.py:180
  271.8 11.2 %project.7 = f32[56,4096]{1,0:T(8,128)S(1)} custom-call(f32[1792,128]{1,0:T(8,128)S(1)} %collective-permute-done.12.refs_0_, f32[1792,128]{1,0:T(8,128)S(1)} %collective-permute-done.13.refs_1_, f32[56,4096]{1,0:T(8,128)S(1)} %pad_maximum_fusion.1.refs_0_.refs_1_.refs_2_, f32[40,4096]{1,0:T(8,128)S(1)} %get-tuple-element.12.refs_1_.refs_2_.refs_3_, ...), custom_call_target="tpu_custom_call" | custom-call | flops 7516192768 | bytes 1835008 | tf_op jit(solution)/shard_map/project/pallas_call | solution.py:180
  283.1 3.1 %collective-permute-done.15 = f32[56,4096]{1,0:T(8,128)S(1)} collective-permute-done((f32[56,4096]{1,0:T(8,128)S(1)}, f32[56,4096]{1,0:T(8,128)S(1)}, u32[]{:S(2)}, u32[]{:S(2)}) %collective-permute-start.15) | collective-permute-done | bytes 917536 | tf_op jit(solution)/shard_map/ppermute | solution.py:24
  (82 shorter events, 41.3 us)
Async XLA Ops:
  0.6 13.9 %copy-start.3 = (f32[54,32,128]{2,1,0:T(8,128)S(1)}, f32[54,32,128]{2,1,0:T(8,128)}, u32[]{:S(2)}) copy-start(f32[54,32,128]{2,1,0:T(8,128)} %param.11) | copy-start | bytes 2654212
  2.4 17.9 %collective-permute-start = (f32[54,1,4,128]{3,2,1,0:T(4,128)}, f32[54,1,4,128]{3,2,1,0:T(4,128)S(1)}, u32[]{:S(2)}, u32[]{:S(2)}) collective-permute-start(f32[54,1,4,128]{3,2,1,0:T(4,128)} %get-tuple-element.26), channel_id=1, source_target_pairs={{4,0},{8,4},{12,8},{16,12},{20,16},{24,20},{28,24},{5,1},{9,5},{13... | collective-permute-start | bytes 331784 | tf_op jit(solution)/shard_map/ppermute | solution.py:19
  3.6 22.5 %collective-permute-start.1 = (f32[54,1,4,128]{3,2,1,0:T(4,128)}, f32[54,1,4,128]{3,2,1,0:T(4,128)S(1)}, u32[]{:S(2)}, u32[]{:S(2)}) collective-permute-start(f32[54,1,4,128]{3,2,1,0:T(4,128)} %get-tuple-element.27), channel_id=1, source_target_pairs={{0,4},{4,8},{8,12},{12,16},{16,20},{20,24},{24,28},{1,5},{5,9},{9,... | collective-permute-start | bytes 331784 | tf_op jit(solution)/shard_map/ppermute | solution.py:19
  11.8 14.3 %collective-permute-start.3 = (f32[54,8,1,128]{3,1,2,0:T(8,128)}, f32[54,8,1,128]{3,1,2,0:T(8,128)S(1)}, u32[]{:S(2)}, u32[]{:S(2)}) collective-permute-start(f32[54,8,1,128]{3,1,2,0:T(8,128)} %bitcast.13), channel_id=1, source_target_pairs={{0,1},{1,2},{2,3},{4,5},{5,6},{6,7},{8,9},{9,10},{10,11},{12,13},{... | collective-permute-start | bytes 663560 | tf_op jit(solution)/shard_map/ppermute | solution.py:19
  13.3 12.9 %collective-permute-start.2 = (f32[54,8,1,128]{3,1,2,0:T(8,128)}, f32[54,8,1,128]{3,1,2,0:T(8,128)S(1)}, u32[]{:S(2)}, u32[]{:S(2)}) collective-permute-start(f32[54,8,1,128]{3,1,2,0:T(8,128)} %bitcast.12), channel_id=1, source_target_pairs={{1,0},{2,1},{3,2},{5,4},{6,5},{7,6},{9,8},{10,9},{11,10},{13,12},{... | collective-permute-start | bytes 663560 | tf_op jit(solution)/shard_map/ppermute | solution.py:19
  16.1 25.9 %collective-permute-start.9 = (f32[54,32,1]{0,1,2:T(8,128)}, f32[54,32,1]{0,1,2:T(8,128)}, u32[]{:S(2)}, u32[]{:S(2)}) collective-permute-start(f32[54,32,1]{0,1,2:T(8,128)} %copy.39), channel_id=1, source_target_pairs={{4,0},{8,4},{12,8},{16,12},{20,16},{24,20},{28,24},{5,1},{9,5},{13... | collective-permute-start | bytes 20744 | tf_op jit(solution)/shard_map/ppermute | solution.py:19
  17.5 8.6 %copy-start.6 = (f32[54,8,4,128]{3,2,1,0:T(4,128)S(1)}, f32[54,8,4,128]{3,2,1,0:T(4,128)}, u32[]{:S(2)}) copy-start(f32[54,8,4,128]{3,2,1,0:T(4,128)} %param.10) | copy-start | bytes 2654212
  17.5 8.6 %copy-start.13 = (f32[54]{0:T(128)S(1)}, f32[54]{0:T(128)}, u32[]{:S(2)}) copy-start(f32[54]{0:T(128)} %param.15) | copy-start | bytes 652
  20.3 19.7 %collective-permute-start.8 = (f32[54,32,1]{0,1,2:T(8,128)}, f32[54,32,1]{0,1,2:T(8,128)}, u32[]{:S(2)}, u32[]{:S(2)}) collective-permute-start(f32[54,32,1]{0,1,2:T(8,128)} %copy.38), channel_id=1, source_target_pairs={{0,4},{4,8},{8,12},{12,16},{16,20},{20,24},{24,28},{1,5},{5,9},{9,... | collective-permute-start | bytes 20744 | tf_op jit(solution)/shard_map/ppermute | solution.py:19
  28.6 7.2 %copy-start.9 = (f32[128,128]{1,0:T(8,128)S(1)}, f32[128,128]{1,0:T(8,128)}, u32[]{:S(2)}) copy-start(f32[128,128]{1,0:T(8,128)} %param.14) | copy-start | bytes 196612
  31.1 24.9 %collective-permute-start.4 = (f32[56,4096]{1,0:T(8,128)S(1)}, f32[56,4096]{1,0:T(8,128)S(1)}, u32[]{:S(2)}, u32[]{:S(2)}) collective-permute-start(f32[56,4096]{1,0:T(8,128)S(1)} %pad_maximum_fusion.1.refs_0_.refs_1_.refs_2_), channel_id=1, source_target_pairs={{0,2},{1,3},{2,0},{3,1},{4,6},{5,7},{6,4},{7,5},{8,10},{9,11},{10,... | collective-permute-start | bytes 2752520 | tf_op jit(solution)/shard_map/ppermute | solution.py:24
  47.0 2.9 collective-permute-start.10
  48.3 3.4 %collective-permute-start.11 = (f32[54,1,128]{2,0,1:T(8,128)S(1)}, f32[54,1,128]{2,0,1:T(8,128)S(1)}, u32[]{:S(2)}, u32[]{:S(2)}) collective-permute-start(f32[54,1,128]{2,0,1:T(8,128)S(1)} %get-tuple-element.21), channel_id=1, source_target_pairs={{1,0},{2,1},{3,2},{5,4},{6,5},{7,6},{9,8},{10,9},{11,10},{13,12},{... | collective-permute-start | bytes 82952 | tf_op jit(solution)/shard_map/ppermute | solution.py:19
  49.9 6.2 %copy-start.5 = (f32[54,4096]{1,0:T(8,128)S(1)}, f32[54,4096]{1,0:T(8,128)}, u32[]{:S(2)}) copy-start(f32[54,4096]{1,0:T(8,128)} %copy-done.4) | copy-start | bytes 2654212
  56.2 33.4 %collective-permute-start.5 = (f32[56,8192]{1,0:T(8,128)S(1)}, f32[56,8192]{1,0:T(8,128)S(1)}, u32[]{:S(2)}, u32[]{:S(2)}) collective-permute-start(f32[56,8192]{1,0:T(8,128)S(1)} %pad_maximum_fusion), channel_id=1, source_target_pairs={{0,1},{1,0},{2,3},{3,2},{4,5},{5,4},{6,7},{7,6},{8,9},{9,8},{10,11... | collective-permute-start | bytes 5505032 | tf_op jit(solution)/shard_map/ppermute | solution.py:24
  112.5 36.5 %collective-permute-start.7 = (f32[1904,128]{1,0:T(8,128)S(1)}, f32[1904,128]{1,0:T(8,128)S(1)}, u32[]{:S(2)}, u32[]{:S(2)}) collective-permute-start(f32[1904,128]{1,0:T(8,128)S(1)} %get-tuple-element.18), channel_id=1, source_target_pairs={{4,0},{8,4},{12,8},{16,12},{20,16},{24,20},{28,24},{5,1},{9,5},{13... | collective-permute-start | bytes 2924552 | tf_op jit(solution)/shard_map/ppermute | solution.py:19
  113.8 45.7 %collective-permute-start.6 = (f32[1904,128]{1,0:T(8,128)S(1)}, f32[1904,128]{1,0:T(8,128)S(1)}, u32[]{:S(2)}, u32[]{:S(2)}) collective-permute-start(f32[1904,128]{1,0:T(8,128)S(1)} %get-tuple-element.19), channel_id=1, source_target_pairs={{0,4},{4,8},{8,12},{12,16},{16,20},{20,24},{24,28},{1,5},{5,9},{9,... | collective-permute-start | bytes 2924552 | tf_op jit(solution)/shard_map/ppermute | solution.py:19
  128.3 31.1 %copy-start = (f32[32,128]{1,0:T(8,128)S(1)}, f32[32,128]{1,0:T(8,128)}, u32[]{:S(2)}) copy-start(f32[32,128]{1,0:T(8,128)} %diss_ref.1) | copy-start | bytes 49156
  128.4 31.1 %copy-start.1 = (f32[32,128]{1,0:T(8,128)S(1)}, f32[32,128]{1,0:T(8,128)}, u32[]{:S(2)}) copy-start(f32[32,128]{1,0:T(8,128)} %rate_ref.1) | copy-start | bytes 49156
  128.4 31.1 %copy-start.2 = (s32[128]{0:T(128)S(1)}, s32[128]{0:T(128)}, u32[]{:S(2)}) copy-start(s32[128]{0:T(128)} %param.19) | copy-start | bytes 1540
  176.2 24.9 %collective-permute-start.13 = (f32[1792,128]{1,0:T(8,128)S(1)}, f32[1792,128]{1,0:T(8,128)S(1)}, u32[]{:S(2)}, u32[]{:S(2)}) collective-permute-start(f32[1792,128]{1,0:T(8,128)S(1)} %bitcast.16), channel_id=1, source_target_pairs={{4,0},{8,4},{12,8},{16,12},{20,16},{24,20},{28,24},{5,1},{9,5},{13... | collective-permute-start | bytes 2752520 | tf_op jit(solution)/shard_map/ppermute | solution.py:19
  177.5 43.5 %collective-permute-start.12 = (f32[1792,128]{1,0:T(8,128)S(1)}, f32[1792,128]{1,0:T(8,128)S(1)}, u32[]{:S(2)}, u32[]{:S(2)}) collective-permute-start(f32[1792,128]{1,0:T(8,128)S(1)} %bitcast.17), channel_id=1, source_target_pairs={{0,4},{4,8},{8,12},{12,16},{16,20},{20,24},{24,28},{1,5},{5,9},{9,... | collective-permute-start | bytes 2752520 | tf_op jit(solution)/shard_map/ppermute | solution.py:19
  243.0 20.3 %collective-permute-start.14 = (f32[56,8192]{1,0:T(8,128)S(1)}, f32[56,8192]{1,0:T(8,128)S(1)}, u32[]{:S(2)}, u32[]{:S(2)}) collective-permute-start(f32[56,8192]{1,0:T(8,128)S(1)} %project.9), channel_id=1, source_target_pairs={{0,1},{1,0},{2,3},{3,2},{4,5},{5,4},{6,7},{7,6},{8,9},{9,8},{10,11... | collective-permute-start | bytes 5505032 | tf_op jit(solution)/shard_map/ppermute | solution.py:24
  263.4 22.8 %collective-permute-start.15 = (f32[56,4096]{1,0:T(8,128)S(1)}, f32[56,4096]{1,0:T(8,128)S(1)}, u32[]{:S(2)}, u32[]{:S(2)}) collective-permute-start(f32[56,4096]{1,0:T(8,128)S(1)} %slice_add_fusion), channel_id=1, source_target_pairs={{0,2},{1,3},{2,0},{3,1},{4,6},{5,7},{6,4},{7,5},{8,10},{9,11},{10,... | collective-permute-start | bytes 2752520 | tf_op jit(solution)/shard_map/ppermute | solution.py:24
  (6 other events, 16.5 us)

commit v2 on v1

--- a/solution.py
+++ b/solution.py
@@ -103,7 +103,7 @@
     if outer:
         shapes.append(jax.ShapeDtypeStruct((wb, count), F32))
         outs.append(col(wb))
-    flops = 4 * rows * width * count
+    flops = rows * width * count // 4
     res = pl.pallas_call(
         functools.partial(bin_kernel, bins, sp, cells, nshape, outer, acc is None),
         grid=(count // ct,),
@@ -119,25 +119,36 @@
 
 
 def chem_kernel(species, sp, own_ref, above_ref, below_ref, moved_ref, diss_ref, rate_ref, count_ref, matrix_ref, out_ref):
-    bins = out_ref.shape[0]
-    matrix = matrix_ref[...]
-    count = count_ref[...]
-    row = lax.broadcasted_iota(jnp.int32, (sp, out_ref.shape[2]), 0)
+    bins, _, cells = out_ref.shape
+    third = matrix_ref.shape[1] // 3
+    high, low = halves(matrix_ref[...])
+    column = lax.broadcasted_iota(jnp.int32, matrix_ref.shape, 1)
+    matrix = jnp.where(column < 2 * third, high.astype(F32), low.astype(F32)).astype(BF16)
+    group = next(g for g in (4, 2, 1) if bins % g == 0)
+    count = jnp.concatenate([count_ref[...]] * group, axis=1)
+    row = lax.broadcasted_iota(jnp.int32, (sp, group * cells), 0)
+    gap = [jnp.zeros((third - sp, group * cells), F32)] * (third > sp)
 
     def blend(b):
         total = own_ref[b] + above_ref[b] + below_ref[b]
         return (total + moved_ref[b]) / (total[species : species + 1, :] + 1.0)
 
-    before, here = blend(0), blend(1)
-    for b in range(bins):
-        after = blend(b + 2)
-        state = here + diss_ref[b : b + 1, :] * (after - 2.0 * here + before)
-        half = 0.5 * rate_ref[b : b + 1, :]
+    def wide(ref, b):
+        return jnp.concatenate([ref[b + n : b + n + 1, :] for n in range(group)], axis=1)
+
+    for b in range(0, bins, group):
+        blends = [blend(b + n) for n in range(group + 2)]
+        before, here, after = (jnp.concatenate(blends[n : n + group], axis=1) for n in range(3))
+        state = here + wide(diss_ref, b) * (after - 2.0 * here + before)
+        half = 0.5 * wide(rate_ref, b)
         for k in range(KMAX):
-            rate = lax.dot_general(matrix, state, NN, precision=lax.Precision.HIGHEST, preferred_element_type=F32)
+            high, low = (part.astype(F32) for part in halves(state))
+            stack = jnp.concatenate([high, *gap, low, *gap, high, *gap], axis=0).astype(BF16)
+            rate = lax.dot_general(matrix, stack, NN, preferred_element_type=F32)
             state = jnp.where(k < count, state + half * jnp.tanh(rate), state)
-        out_ref[b] = jnp.where(row == species, 1.0, state)
-        before, here = here, after
+        state = jnp.where(row == species, 1.0, state)
+        for n in range(group):
+            out_ref[b + n] = state[:, n * cells : (n + 1) * cells]
 
 
 def project_kernel(bins, sp, cells, nshape, groups, accumulate, *refs):
@@ -185,7 +196,7 @@
         out_specs=col(sp),
         scratch_shapes=[pltpu.VMEM((rows, 2 * len(groups) * cells), BF16)],
         compiler_params=pltpu.CompilerParams(vmem_limit_bytes=40 << 20),
-        cost_estimate=pl.CostEstimate(flops=4 * rows * cells * len(groups) * count, bytes_accessed=8 * sp * count, transcendentals=0),
+        cost_estimate=pl.CostEstimate(flops=rows * cells * len(groups) * count // 4, bytes_accessed=8 * sp * count, transcendentals=0),
         name="project",
     )(*args)
 
@@ -222,21 +233,7 @@
     used = lax.broadcasted_iota(jnp.int32, (wb, 1), 0) < bins
     table = jnp.where(used, table, 0.0)
 
-    blocks = [t_own]
-    bits = [1 << k for k in range(ncross.bit_length() - 1)][::-1]
-    for bit in bits:
-        blocks.append(swap(jnp.concatenate(blocks, axis=1) if len(blocks) > 1 else blocks[0], "cross", bit))
-
-    acc, wcs = None, []
-    for block in blocks:
-        acc, wc = bin_call(block, table, None, acc, bins, cells, nshape)
-        wcs.append(wc)
-    up = shift(acc[:, cells:], "slab", 1)
-    down = shift(acc[:, :cells], "slab", -1)
-    mine = None
-    for block, wc in zip(blocks, wcs):
-        mine = bin_call(block, table, wc, mine, bins, cells, nshape)
-
+    cmc_state, t_own = lax.optimization_barrier((cmc_state, t_own))
     left_cells = jnp.concatenate([shift(cmc_state[:, :, -1:], "slab", 1), cmc_state[:, :, :-1]], axis=2)
     right_cells = jnp.concatenate([cmc_state[:, :, 1:], shift(cmc_state[:, :, :1], "slab", -1)], axis=2)
     moved = cmc_state - 0.4 * (cmc_state - left_cells) + 0.1 * (right_cells - 2.0 * cmc_state + left_cells)
@@ -244,6 +241,25 @@
         [shift(moved[:, -1:], "cross", 1), moved, shift(moved[:, :1], "cross", -1)], axis=1
     )
     moved = jnp.pad(moved.transpose(1, 0, 2), ((0, 0), (0, sp - species), (0, 0)))
+
+    blocks = [t_own]
+    bits = [1 << k for k in range(ncross.bit_length() - 1)][::-1]
+    for bit in bits:
+        got = swap(jnp.concatenate(blocks, axis=1) if len(blocks) > 1 else blocks[0], "cross", bit)
+        if len(blocks) == 1:
+            got, moved = lax.optimization_barrier((got, moved))
+        blocks.append(got)
+
+    acc, wcs = None, []
+    for block in blocks:
+        acc, wc = bin_call(block, table, None, acc, bins, cells, nshape)
+        wcs.append(wc)
+    up = shift(acc[:, cells:], "slab", 1)
+    down = shift(acc[:, :cells], "slab", -1)
+    acc, *wcs = lax.optimization_barrier((acc, *wcs))
+    mine = None
+    for block, wc in zip(blocks, wcs):
+        mine = bin_call(block, table, wc, mine, bins, cells, nshape)
 
     cube = lambda a: a.reshape(bins, sp, cells)
     extra = sp - species
@@ -254,7 +270,7 @@
         name="chem",
     )(
         cube(mine), cube(up), cube(down), moved, dissipation, reaction_rate, substeps[None, :],
-        jnp.pad(chem_matrix, ((0, extra), (0, extra))),
+        jnp.tile(jnp.pad(chem_matrix, ((0, extra), (0, -(-sp // 16) * 16 - species))), (1, 3)),
     )
     cmc_out = fresh[:, :species].transpose(1, 0, 2)
     fresh = fresh.reshape(own_bins * sp, cells)
@@ -263,6 +279,7 @@
 
     args = (own_bins, cells, nshape)
     own_part = [project_call([fresh], (1,), b, w, None, *args) for b, w in zip(blocks, wcs)]
+    from_below, from_above, *own_part = lax.optimization_barrier((from_below, from_above, *own_part))
     parts = [None] * len(blocks)
     for n in reversed(range(len(blocks))):
         parts[n] = project_call([from_below, from_above], (0, 2), blocks[n], wcs[n], own_part[n], *args)

time: 291 us -> 265 us (0.911)
  waiting for transfers between devices: 42.3 us -> 24 us
  Pallas kernels: 179 us -> 167 us
    ppermute x12, waiting for transfers between devices: 34.9 us -> 14.4 us  [shift(): lax.ppermute(array, axis, [(i, i + by) for i in range(count) if 0 <= i +...]
    pallas_call x1, Pallas kernels: 16.7 us -> 6.01 us  [on_device(): pl.pallas_call(functools.partial(chem_kernel, species, sp), out_shape=jax...]
    unnamed x34 -> x54, local copies, waits for them, and re-layouts: 9.13 us -> 4.4 us
    optimization_barrier x0 -> x2, local copies, waits for them, and re-layouts: none -> 3.45 us  [on_device(): cmc_state, t_own = lax.optimization_barrier((cmc_state, t_own))]
  transfers between devices with their start and end apart: 16 -> 16, of which waited for: 6 -> 5; matrix products, arithmetic and copies ran while one was open for 8% -> 6% of each run, Pallas kernels for 40% -> 44%
where the time goes in v2:
time: 265 us; the launch traced here: 264 us
  Pallas kernels  167 us (63%)
  starting transfers between devices  38.3 us (14%)
  waiting for transfers between devices  24 us (9%)
  local copies, waits for them, and re-layouts  22.4 us (8%)
  other arithmetic  11.1 us (4%)
    pallas_call x6, Pallas kernels, bin_call(): pl.pallas_call(functools.partial(bin_kernel, bins, sp, cells, nshape, out...  85.2 us
    pallas_call x6, Pallas kernels, project_call(): pl.pallas_call(functools.partial(project_kernel, bins, sp, cells, nshape,...  75.4 us
    ppermute x12, starting transfers between devices, shift(): lax.ppermute(array, axis, [(i, i + by) for i in range(count) if 0 <= i +...  30.6 us
    ppermute x12, waiting for transfers between devices, shift(): lax.ppermute(array, axis, [(i, i + by) for i in range(count) if 0 <= i +...  14.4 us
    ppermute x4, waiting for transfers between devices, swap(): return lax.ppermute(array, axis, [(i, i ^ bit) for i in range(count)])  9.61 us
    ppermute x4, starting transfers between devices, swap(): return lax.ppermute(array, axis, [(i, i ^ bit) for i in range(count)])  7.67 us
    pallas_call x1, Pallas kernels, on_device(): pl.pallas_call(functools.partial(chem_kernel, species, sp), out_shape=jax...  6.01 us
  transfers between devices with their start and end apart: 16, of which 5 were waited for; matrix products, arithmetic and copies ran while one was open for 6% of the time, Pallas kernels for 44%

profile of v2, /device:TPU:0, one launch (start us, length us, event | category | flops | bytes accessed | tf_op | source)
XLA Modules:
  0.0 263.7 jit_solution(17690998747054253504)
XLA Ops:
  3.0 5.5 %collective-permute-start.1 = (f32[54,1,4,128]{3,2,1,0:T(4,128)S(1)}, f32[54,1,4,128]{3,2,1,0:T(4,128)S(1)}, u32[]{:S(2)}, u32[]{:S(2)}) collective-permute-start(f32[54,1,4,128]{3,2,1,0:T(4,128)S(1)} %get-tuple-element.53), channel_id=1, source_target_pairs={{0,4},{4,8},{8,12},{12,16},{16,20},{20,24},{24,28},{1,5},{5,9},{9,... | collective-permute-start | bytes 331784 | tf_op jit(solution)/shard_map/ppermute | solution.py:19
  14.0 3.3 %collective-permute-done.2 = f32[54,8,1,128]{3,1,2,0:T(8,128)S(1)} collective-permute-done((f32[54,8,1,128]{3,1,2,0:T(8,128)S(1)}, f32[54,8,1,128]{3,1,2,0:T(8,128)S(1)}, u32[]{:S(2)}, u32[]{:S(2)}) %collective-permute-start.2) | collective-permute-done | bytes 221216 | tf_op jit(solution)/shard_map/ppermute | solution.py:19
  18.1 3.1 %fusion.8 = f32[54,8,4,128]{3,2,1,0:T(4,128)} fusion(f32[54,8,4,128]{3,2,1,0:T(4,128)S(1)} %copy-done.13, f32[54,8,1,128]{3,2,1,0:T(1,128)S(1)} %bitcast.24, f32[54,8,1,128]{3,2,1,0:T(1,128)S(1)} %bitcast.26, f32[54,1,4,128]{3,2,1,0:T(4,128)S(1)} %collective-permute-done.1, f32[54,1,4,128]{3,2,1,0:T(4,128)S(1)} %collective-permute-done, f32[54]{0:T(128)} %param.15), kind=kLoop, calls=%fused_computation.19 | loop fusion | flops 2875392 | bytes 2433240 | tf_op jit(solution)/shard_map/add | solution.py:223
  23.4 2.9 %copy.34 = f32[54,32,128]{0,1,2:T(8,128)} copy(f32[54,32,128]{2,1,0:T(8,128)S(1)} %copy-done.11) | data formatting | bytes 1769472 | tf_op jit(solution)/shard_map/optimization_barrier | solution.py:236
  26.3 4.1 %collective-permute-start.4 = (f32[56,4096]{1,0:T(8,128)S(1)}, f32[56,4096]{1,0:T(8,128)S(1)}, u32[]{:S(2)}, u32[]{:S(2)}) collective-permute-start(f32[56,4096]{1,0:T(8,128)S(1)} %pad_maximum_fusion.1.refs_0_.refs_1_.refs_2_), channel_id=1, source_target_pairs={{0,2},{1,3},{2,0},{3,1},{4,6},{5,7},{6,4},{7,5},{8,10},{9,11},{10,... | collective-permute-start | bytes 2752520 | tf_op jit(solution)/shard_map/ppermute | solution.py:24
  31.2 4.3 %collective-permute-start.5 = (f32[54,32,1]{0,1,2:T(8,128)S(1)}, f32[54,32,1]{0,1,2:T(8,128)S(1)}, u32[]{:S(2)}, u32[]{:S(2)}) collective-permute-start(f32[54,32,1]{0,1,2:T(8,128)S(1)} %get-tuple-element.44), channel_id=1, source_target_pairs={{0,4},{4,8},{8,12},{12,16},{16,20},{20,24},{24,28},{1,5},{5,9},{9,... | collective-permute-start | bytes 20744 | tf_op jit(solution)/shard_map/ppermute | solution.py:19
  43.8 2.9 %fusion.3 = f32[54,32,128]{2,0,1:T(8,128)S(1)} fusion(f32[54,32,1]{2,0,1:T(8,128)} %copy.41, f32[54,32,127]{2,0,1:T(8,128)} %get-tuple-element.51, f32[54,32,127]{2,0,1:T(8,128)} %get-tuple-element.50, f32[54,32,1]{2,0,1:T(8,128)} %copy.36, f32[54,32,128]{2,1,0:T(8,128)S(1)} %copy-done.12), kind=kLoop, calls=%fused_computation.14 | loop fusion | flops 2211840 | bytes 3538944 | tf_op jit(solution)/shard_map/add | solution.py:239
  57.5 11.4 %bin_outer.3 = (f32[1904,256]{1,0:T(8,128)S(1)}, f32[40,4096]{1,0:T(8,128)S(1)}) custom-call(f32[56,4096]{1,0:T(8,128)S(1)} %pad_maximum_fusion.1.refs_0_.refs_1_.refs_2_, f32[40,128]{1,0:T(8,128)S(1)} %fusion.12.refs_1_), custom_call_target="tpu_custom_call" | custom-call | flops 499122176 | bytes 917504 | tf_op jit(solution)/shard_map/bin_outer/pallas_call | solution.py:107
  69.0 11.4 %bin_outer.4 = (f32[1904,256]{1,0:T(8,128)S(1)}, f32[40,4096]{1,0:T(8,128)S(1)}) custom-call(f32[56,4096]{1,0:T(8,128)S(1)} %copy-done.1, f32[40,128]{1,0:T(8,128)S(1)} %fusion.12.refs_1_, f32[1904,256]{1,0:T(8,128)S(1)} %get-tuple-element.23.refs_2_), custom_call_target="tpu_custom_call" | custom-call | flops 499122176 | bytes 917504 | tf_op jit(solution)/shard_map/bin_outer/pallas_call | solution.py:107
  81.2 22.6 %bin_outer.5 = (f32[1904,256]{1,0:T(8,128)S(1)}, f32[40,8192]{1,0:T(8,128)S(1)}) custom-call(f32[56,8192]{1,0:T(8,128)S(1)} %collective-permute-done.9.refs_0_.refs_1_.refs_2_, f32[40,128]{1,0:T(8,128)S(1)} %fusion.12.refs_1_, f32[1904,256]{1,0:T(8,128)S(1)} %get-tuple-element.24.refs_2_), custom_call_target="tpu_custom_call" | custom-call | flops 998244352 | bytes 1835008 | tf_op jit(solution)/shard_map/bin_outer/pallas_call | solution.py:107
  106.8 5.5 %collective-permute-start.10 = (f32[1904,128]{1,0:T(8,128)}, f32[1904,128]{1,0:T(8,128)}, u32[]{:S(2)}, u32[]{:S(2)}) collective-permute-start(f32[1904,128]{1,0:T(8,128)} %get-tuple-element.47), channel_id=1, source_target_pairs={{0,4},{4,8},{8,12},{12,16},{16,20},{20,24},{24,28},{1,5},{5,9},{9,... | collective-permute-start | bytes 2924552 | tf_op jit(solution)/shard_map/ppermute | solution.py:19
  114.1 9.9 %bin_own.3.refs_2_ = f32[1904,128]{1,0:T(8,128)S(1)} custom-call(f32[56,4096]{1,0:T(8,128)S(1)} %pad_maximum_fusion.1.refs_0_.refs_1_.refs_2_, f32[40,4096]{1,0:T(8,128)S(1)} %get-tuple-element.31.refs_1_.refs_2_.refs_3_), custom_call_target="tpu_custom_call" | custom-call | flops 249561088 | bytes 917504 | tf_op jit(solution)/shard_map/bin_own/pallas_call | solution.py:107
  124.0 10.1 %bin_own.4.refs_2_ = f32[1904,128]{1,0:T(8,128)S(1)} custom-call(f32[56,4096]{1,0:T(8,128)S(1)} %copy-done.2, f32[40,4096]{1,0:T(8,128)S(1)} %copy-done.6, f32[1904,128]{1,0:T(8,128)S(1)} %bin_own.3.refs_2_), custom_call_target="tpu_custom_call" | custom-call | flops 249561088 | bytes 917504 | tf_op jit(solution)/shard_map/bin_own/pallas_call | solution.py:107
  134.2 19.7 %bin_own.5 = f32[1904,128]{1,0:T(8,128)S(1)} custom-call(f32[56,8192]{1,0:T(8,128)S(1)} %collective-permute-done.9.refs_0_.refs_1_.refs_2_, f32[40,8192]{1,0:T(8,128)S(1)} %copy-done.4, f32[1904,128]{1,0:T(8,128)S(1)} %bin_own.4.refs_2_), custom_call_target="tpu_custom_call" | custom-call | flops 499122176 | bytes 1835008 | tf_op jit(solution)/shard_map/bin_own/pallas_call | solution.py:107
  154.0 6.0 %chem.1 = f32[32,56,128]{2,1,0:T(8,128)S(1)} custom-call(f32[34,56,128]{2,1,0:T(8,128)S(1)} %bitcast.22, f32[34,56,128]{2,1,0:T(8,128)} %bitcast.6.above_ref, f32[34,56,128]{2,1,0:T(8,128)} %bitcast.7.below_ref, f32[34,56,128]{2,1,0:T(8,128)S(1)} %copy-done.7, f32[32,128]{1,0:T(8,128)S(1)} %copy-done.8, f32[32,128]{1,0:T(8,128)S(1)} %copy-done.9, ...), custom_call_target="tpu_custom_call" | custom-call | tf_op jit(solution)/shard_map/chem/pallas_call | solution.py:266
  161.3 4.8 %collective-permute-start.12 = (f32[1792,128]{1,0:T(8,128)S(1)}, f32[1792,128]{1,0:T(8,128)S(1)}, u32[]{:S(2)}, u32[]{:S(2)}) collective-permute-start(f32[1792,128]{1,0:T(8,128)S(1)} %bitcast.18), channel_id=1, source_target_pairs={{0,4},{4,8},{8,12},{12,16},{16,20},{20,24},{24,28},{1,5},{5,9},{9,... | collective-permute-start | bytes 2752520 | tf_op jit(solution)/shard_map/ppermute | solution.py:19
  166.1 7.8 %project.7.refs_4_ = f32[56,4096]{1,0:T(8,128)S(1)} custom-call(f32[1792,128]{1,0:T(8,128)S(1)} %bitcast.19, f32[56,4096]{1,0:T(8,128)S(1)} %copy-done.2, f32[40,4096]{1,0:T(8,128)S(1)} %copy-done.6), custom_call_target="tpu_custom_call" | custom-call | flops 234881024 | bytes 1835008 | tf_op jit(solution)/shard_map/project/pallas_call | solution.py:191
  173.9 7.8 %project.6.refs_4_ = f32[56,4096]{1,0:T(8,128)S(1)} custom-call(f32[1792,128]{1,0:T(8,128)S(1)} %bitcast.20, f32[56,4096]{1,0:T(8,128)S(1)} %pad_maximum_fusion.1.refs_0_.refs_1_.refs_2_, f32[40,4096]{1,0:T(8,128)S(1)} %get-tuple-element.31.refs_1_.refs_2_.refs_3_), custom_call_target="tpu_custom_call" | custom-call | flops 234881024 | bytes 1835008 | tf_op jit(solution)/shard_map/project/pallas_call | solution.py:191
  181.7 15.4 %project.8.refs_4_ = f32[56,8192]{1,0:T(8,128)S(1)} custom-call(f32[1792,128]{1,0:T(8,128)S(1)} %bitcast.21, f32[56,8192]{1,0:T(8,128)S(1)} %collective-permute-done.9.refs_0_.refs_1_.refs_2_, f32[40,8192]{1,0:T(8,128)S(1)} %copy-done.4), custom_call_target="tpu_custom_call" | custom-call | flops 469762048 | bytes 3670016 | tf_op jit(solution)/shard_map/project/pallas_call | solution.py:191
  197.2 6.3 %collective-permute-done.12.refs_0_ = f32[1792,128]{1,0:T(8,128)S(1)} collective-permute-done((f32[1792,128]{1,0:T(8,128)S(1)}, f32[1792,128]{1,0:T(8,128)S(1)}, u32[]{:S(2)}, u32[]{:S(2)}) %collective-permute-start.12) | collective-permute-done | bytes 917536 | tf_op jit(solution)/shard_map/ppermute | solution.py:19
  203.4 22.0 %project.10 = f32[56,8192]{1,0:T(8,128)S(1)} custom-call(f32[1792,128]{1,0:T(8,128)S(1)} %collective-permute-done.12.refs_0_, f32[1792,128]{1,0:T(8,128)S(1)} %collective-permute-done.13.refs_1_, f32[56,8192]{1,0:T(8,128)S(1)} %collective-permute-done.9.refs_0_.refs_1_.refs_2_, f32[40,8192]{1,0:T(8,128)S(1)} %copy-done.4, f32[56,8192]{1,0:T(8,128)S(1)} %project.8.refs_4_), custom_call_target="tpu_custom_call" | custom-call | flops 939524096 | bytes 3670016 | tf_op jit(solution)/shard_map/project/pallas_call | solution.py:191
  225.6 11.2 %project.11 = f32[56,4096]{1,0:T(8,128)S(1)} custom-call(f32[1792,128]{1,0:T(8,128)S(1)} %collective-permute-done.12.refs_0_, f32[1792,128]{1,0:T(8,128)S(1)} %collective-permute-done.13.refs_1_, f32[56,4096]{1,0:T(8,128)S(1)} %copy-done.2, f32[40,4096]{1,0:T(8,128)S(1)} %copy-done.6, f32[56,4096]{1,0:T(8,128)S(1)} %project.7.refs_4_), custom_call_target="tpu_custom_call" | custom-call | flops 469762048 | bytes 1835008 | tf_op jit(solution)/shard_map/project/pallas_call | solution.py:191
  238.9 11.2 %project.9 = f32[56,4096]{1,0:T(8,128)S(1)} custom-call(f32[1792,128]{1,0:T(8,128)S(1)} %collective-permute-done.12.refs_0_, f32[1792,128]{1,0:T(8,128)S(1)} %collective-permute-done.13.refs_1_, f32[56,4096]{1,0:T(8,128)S(1)} %pad_maximum_fusion.1.refs_0_.refs_1_.refs_2_, f32[40,4096]{1,0:T(8,128)S(1)} %get-tuple-element.31.refs_1_.refs_2_.refs_3_, ...), custom_call_target="tpu_custom_call" | custom-call | flops 469762048 | bytes 1835008 | tf_op jit(solution)/shard_map/project/pallas_call | solution.py:191
  250.1 9.6 %collective-permute-done.15 = f32[56,4096]{1,0:T(8,128)S(1)} collective-permute-done((f32[56,4096]{1,0:T(8,128)S(1)}, f32[56,4096]{1,0:T(8,128)S(1)}, u32[]{:S(2)}, u32[]{:S(2)}) %collective-permute-start.15) | collective-permute-done | bytes 917536 | tf_op jit(solution)/shard_map/ppermute | solution.py:24
  (106 shorter events, 43.6 us)
Async XLA Ops:
  0.6 17.4 %copy-start.13 = (f32[54,8,4,128]{3,2,1,0:T(4,128)S(1)}, f32[54,8,4,128]{3,2,1,0:T(4,128)}, u32[]{:S(2)}) copy-start(f32[54,8,4,128]{3,2,1,0:T(4,128)} %param.10) | copy-start | bytes 2654212
  1.7 12.3 %collective-permute-start = (f32[54,1,4,128]{3,2,1,0:T(4,128)S(1)}, f32[54,1,4,128]{3,2,1,0:T(4,128)S(1)}, u32[]{:S(2)}, u32[]{:S(2)}) collective-permute-start(f32[54,1,4,128]{3,2,1,0:T(4,128)S(1)} %get-tuple-element.52), channel_id=1, source_target_pairs={{4,0},{8,4},{12,8},{16,12},{20,16},{24,20},{28,24},{5,1},{9,5},{13... | collective-permute-start | bytes 331784 | tf_op jit(solution)/shard_map/ppermute | solution.py:19
  3.0 11.0 %collective-permute-start.1 = (f32[54,1,4,128]{3,2,1,0:T(4,128)S(1)}, f32[54,1,4,128]{3,2,1,0:T(4,128)S(1)}, u32[]{:S(2)}, u32[]{:S(2)}) collective-permute-start(f32[54,1,4,128]{3,2,1,0:T(4,128)S(1)} %get-tuple-element.53), channel_id=1, source_target_pairs={{0,4},{4,8},{8,12},{12,16},{16,20},{20,24},{24,28},{1,5},{5,9},{9,... | collective-permute-start | bytes 331784 | tf_op jit(solution)/shard_map/ppermute | solution.py:19
  10.4 3.6 %collective-permute-start.3 = (f32[54,8,1,128]{3,1,2,0:T(8,128)S(1)}, f32[54,8,1,128]{3,1,2,0:T(8,128)S(1)}, u32[]{:S(2)}, u32[]{:S(2)}) collective-permute-start(f32[54,8,1,128]{3,1,2,0:T(8,128)S(1)} %bitcast.30), channel_id=1, source_target_pairs={{0,1},{1,2},{2,3},{4,5},{5,6},{6,7},{8,9},{9,10},{10,11},{12,13},{... | collective-permute-start | bytes 663560 | tf_op jit(solution)/shard_map/ppermute | solution.py:19
  11.9 5.5 %collective-permute-start.2 = (f32[54,8,1,128]{3,1,2,0:T(8,128)S(1)}, f32[54,8,1,128]{3,1,2,0:T(8,128)S(1)}, u32[]{:S(2)}, u32[]{:S(2)}) collective-permute-start(f32[54,8,1,128]{3,1,2,0:T(8,128)S(1)} %bitcast.29), channel_id=1, source_target_pairs={{1,0},{2,1},{3,2},{5,4},{6,5},{7,6},{9,8},{10,9},{11,10},{13,12},{... | collective-permute-start | bytes 663560 | tf_op jit(solution)/shard_map/ppermute | solution.py:19
  26.3 26.1 %collective-permute-start.4 = (f32[56,4096]{1,0:T(8,128)S(1)}, f32[56,4096]{1,0:T(8,128)S(1)}, u32[]{:S(2)}, u32[]{:S(2)}) collective-permute-start(f32[56,4096]{1,0:T(8,128)S(1)} %pad_maximum_fusion.1.refs_0_.refs_1_.refs_2_), channel_id=1, source_target_pairs={{0,2},{1,3},{2,0},{3,1},{4,6},{5,7},{6,4},{7,5},{8,10},{9,11},{10,... | collective-permute-start | bytes 2752520 | tf_op jit(solution)/shard_map/ppermute | solution.py:24
  31.2 11.3 %collective-permute-start.5 = (f32[54,32,1]{0,1,2:T(8,128)S(1)}, f32[54,32,1]{0,1,2:T(8,128)S(1)}, u32[]{:S(2)}, u32[]{:S(2)}) collective-permute-start(f32[54,32,1]{0,1,2:T(8,128)S(1)} %get-tuple-element.44), channel_id=1, source_target_pairs={{0,4},{4,8},{8,12},{12,16},{16,20},{20,24},{24,28},{1,5},{5,9},{9,... | collective-permute-start | bytes 20744 | tf_op jit(solution)/shard_map/ppermute | solution.py:19
  35.5 5.6 %collective-permute-start.6 = (f32[54,32,1]{0,1,2:T(8,128)S(1)}, f32[54,32,1]{0,1,2:T(8,128)S(1)}, u32[]{:S(2)}, u32[]{:S(2)}) collective-permute-start(f32[54,32,1]{0,1,2:T(8,128)S(1)} %get-tuple-element.45), channel_id=1, source_target_pairs={{4,0},{8,4},{12,8},{16,12},{20,16},{24,20},{28,24},{5,1},{9,5},{13... | collective-permute-start | bytes 20744 | tf_op jit(solution)/shard_map/ppermute | solution.py:19
  46.7 2.6 collective-permute-start.7
  48.0 3.3 %collective-permute-start.8 = (f32[54,1,128]{2,0,1:T(8,128)S(1)}, f32[54,1,128]{2,0,1:T(8,128)S(1)}, u32[]{:S(2)}, u32[]{:S(2)}) collective-permute-start(f32[54,1,128]{2,0,1:T(8,128)S(1)} %get-tuple-element.49), channel_id=1, source_target_pairs={{1,0},{2,1},{3,2},{5,4},{6,5},{7,6},{9,8},{10,9},{11,10},{13,12},{... | collective-permute-start | bytes 82952 | tf_op jit(solution)/shard_map/ppermute | solution.py:19
  54.7 26.5 %collective-permute-start.9 = (f32[56,8192]{1,0:T(8,128)}, f32[56,8192]{1,0:T(8,128)S(1)}, u32[]{:S(2)}, u32[]{:S(2)}) collective-permute-start(f32[56,8192]{1,0:T(8,128)} %pad_maximum_fusion), channel_id=1, source_target_pairs={{0,1},{1,0},{2,3},{3,2},{4,5},{5,4},{6,7},{7,6},{8,9},{9,8},{10,11... | collective-permute-start | bytes 5505032 | tf_op jit(solution)/shard_map/ppermute | solution.py:24
  57.4 11.5 %copy-start.1 = (f32[56,4096]{1,0:T(8,128)S(1)}, f32[56,4096]{1,0:T(8,128)}, u32[]{:S(2)}) copy-start(f32[56,4096]{1,0:T(8,128)} %copy-done) | copy-start | bytes 2752516
  105.6 48.4 %collective-permute-start.11 = (f32[1904,128]{1,0:T(8,128)}, f32[1904,128]{1,0:T(8,128)}, u32[]{:S(2)}, u32[]{:S(2)}) collective-permute-start(f32[1904,128]{1,0:T(8,128)} %get-tuple-element.46), channel_id=1, source_target_pairs={{4,0},{8,4},{12,8},{16,12},{20,16},{24,20},{28,24},{5,1},{9,5},{13... | collective-permute-start | bytes 2924552 | tf_op jit(solution)/shard_map/ppermute | solution.py:19
  106.8 47.1 %collective-permute-start.10 = (f32[1904,128]{1,0:T(8,128)}, f32[1904,128]{1,0:T(8,128)}, u32[]{:S(2)}, u32[]{:S(2)}) collective-permute-start(f32[1904,128]{1,0:T(8,128)} %get-tuple-element.47), channel_id=1, source_target_pairs={{0,4},{4,8},{8,12},{12,16},{16,20},{20,24},{24,28},{1,5},{5,9},{9,... | collective-permute-start | bytes 2924552 | tf_op jit(solution)/shard_map/ppermute | solution.py:19
  114.1 9.9 %copy-start.6 = (f32[40,4096]{1,0:T(8,128)S(1)}, f32[40,4096]{1,0:T(8,128)}, u32[]{:S(2)}) copy-start(f32[40,4096]{1,0:T(8,128)} %copy-done.5) | copy-start | bytes 1966084
  124.0 10.1 %copy-start.4 = (f32[40,8192]{1,0:T(8,128)S(1)}, f32[40,8192]{1,0:T(8,128)}, u32[]{:S(2)}) copy-start(f32[40,8192]{1,0:T(8,128)} %copy-done.3) | copy-start | bytes 3932164
  134.1 19.8 %copy-start.7 = (f32[34,56,128]{2,1,0:T(8,128)S(1)}, f32[34,56,128]{2,1,0:T(8,128)}, u32[]{:S(2)}) copy-start(f32[34,56,128]{2,1,0:T(8,128)} %pad.17.moved_ref) | copy-start | bytes 2924548
  134.1 19.8 %copy-start.8 = (f32[32,128]{1,0:T(8,128)S(1)}, f32[32,128]{1,0:T(8,128)}, u32[]{:S(2)}) copy-start(f32[32,128]{1,0:T(8,128)} %diss_ref.1) | copy-start | bytes 49156
  134.2 19.8 %copy-start.9 = (f32[32,128]{1,0:T(8,128)S(1)}, f32[32,128]{1,0:T(8,128)}, u32[]{:S(2)}) copy-start(f32[32,128]{1,0:T(8,128)} %rate_ref.1) | copy-start | bytes 49156
  134.2 19.8 %copy-start.10 = (s32[128]{0:T(128)S(1)}, s32[128]{0:T(128)}, u32[]{:S(2)}) copy-start(s32[128]{0:T(128)} %param.19) | copy-start | bytes 1540
  160.0 37.2 %collective-permute-start.13 = (f32[1792,128]{1,0:T(8,128)S(1)}, f32[1792,128]{1,0:T(8,128)S(1)}, u32[]{:S(2)}, u32[]{:S(2)}) collective-permute-start(f32[1792,128]{1,0:T(8,128)S(1)} %bitcast.17), channel_id=1, source_target_pairs={{4,0},{8,4},{12,8},{16,12},{20,16},{24,20},{28,24},{5,1},{9,5},{13... | collective-permute-start | bytes 2752520 | tf_op jit(solution)/shard_map/ppermute | solution.py:19
  161.3 42.2 %collective-permute-start.12 = (f32[1792,128]{1,0:T(8,128)S(1)}, f32[1792,128]{1,0:T(8,128)S(1)}, u32[]{:S(2)}, u32[]{:S(2)}) collective-permute-start(f32[1792,128]{1,0:T(8,128)S(1)} %bitcast.18), channel_id=1, source_target_pairs={{0,4},{4,8},{8,12},{12,16},{16,20},{20,24},{24,28},{1,5},{5,9},{9,... | collective-permute-start | bytes 2752520 | tf_op jit(solution)/shard_map/ppermute | solution.py:19
  225.5 11.3 %collective-permute-start.14 = (f32[56,8192]{1,0:T(8,128)S(1)}, f32[56,8192]{1,0:T(8,128)S(1)}, u32[]{:S(2)}, u32[]{:S(2)}) collective-permute-start(f32[56,8192]{1,0:T(8,128)S(1)} %project.10), channel_id=1, source_target_pairs={{0,1},{1,0},{2,3},{3,2},{4,5},{5,4},{6,7},{7,6},{8,9},{9,8},{10,11... | collective-permute-start | bytes 5505032 | tf_op jit(solution)/shard_map/ppermute | solution.py:24
  236.9 22.9 %collective-permute-start.15 = (f32[56,4096]{1,0:T(8,128)S(1)}, f32[56,4096]{1,0:T(8,128)S(1)}, u32[]{:S(2)}, u32[]{:S(2)}) collective-permute-start(f32[56,4096]{1,0:T(8,128)S(1)} %slice_add_fusion), channel_id=1, source_target_pairs={{0,2},{1,3},{2,0},{3,1},{4,6},{5,7},{6,4},{7,5},{8,10},{9,11},{10,... | collective-permute-start | bytes 2752520 | tf_op jit(solution)/shard_map/ppermute | solution.py:24
  (18 other events, 52.2 us)

commit v3 on v2

--- a/solution.py
+++ b/solution.py
@@ -178,13 +178,15 @@
     out_ref[...] = total
 
 
-def project_call(xs, groups, t, wc, acc, bins, cells, nshape, ct=256):
-    sp, count = t.shape
+def project_call(xs, groups, t, wc, acc, place, count, bins, cells, nshape, ct=256):
+    sp, skip = t.shape[0], place // ct
     rows = bins * sp
     whole = lambda shape: pl.BlockSpec(shape, lambda i: (0,) * len(shape))
     col = lambda r: pl.BlockSpec((r, ct), lambda i: (0, i))
     args = list(xs) + [t, wc]
-    specs = [whole(x.shape) for x in xs] + [pl.BlockSpec((8, ct), lambda i: (sp // 8 - 1, i)), col(wc.shape[0])]
+    specs = [whole(x.shape) for x in xs]
+    specs.append(pl.BlockSpec((8, ct), lambda i: (sp // 8 - 1, i + skip)))
+    specs.append(pl.BlockSpec((wc.shape[0], ct), lambda i: (0, i + skip)))
     if acc is not None:
         args.append(acc)
         specs.append(col(sp))
@@ -212,10 +214,29 @@
     count = cmc_map.size
     ncross = lax.axis_size("cross")
 
-    below = shift(les_state[:, -1:], "slab", 1)
-    above = shift(les_state[:, :1], "slab", -1)
-    behind = shift(les_state[:, :, -1:], "cross", 1)
-    ahead = shift(les_state[:, :, :1], "cross", -1)
+    planes, ends = les_state.shape[1], les_state.shape[2] * les_state.shape[3]
+
+    def slab_end(at):
+        return jnp.concatenate([les_state[:, at].reshape(species, ends), cmc_state[:, :, at]], axis=1)
+
+    from_left, from_right = shift(slab_end(-1), "slab", 1), shift(slab_end(0), "slab", -1)
+    below, above = (g[:, :ends].reshape(les_state[:, :1].shape) for g in (from_left, from_right))
+    left_end, right_end = from_left[:, ends:, None], from_right[:, ends:, None]
+
+    def advect(state, left, right):
+        left = jnp.concatenate([left, state[:, :, :-1]], axis=2)
+        right = jnp.concatenate([state[:, :, 1:], right], axis=2)
+        return state - 0.4 * (state - left) + 0.1 * (right - 2.0 * state + left)
+
+    def cross_end(at):
+        rows = les_state[:, :, at].reshape(species, -1)
+        pick = slice(at, at + 1 or None)
+        bin_row = advect(cmc_state[:, pick], left_end[:, pick], right_end[:, pick])
+        return jnp.concatenate([rows, bin_row[:, 0]], axis=1)
+
+    from_behind, from_ahead = shift(cross_end(-1), "cross", 1), shift(cross_end(0), "cross", -1)
+    behind, ahead = (g[:, :-cells].reshape(les_state[:, :, :1].shape) for g in (from_behind, from_ahead))
+    bin_before, bin_after = from_behind[:, None, -cells:], from_ahead[:, None, -cells:]
     xs = jnp.concatenate([below, les_state, above], axis=1)
     ys = jnp.concatenate([behind, les_state, ahead], axis=2)
     zs = jnp.pad(les_state, ((0, 0), (0, 0), (0, 0), (1, 1)))
@@ -234,24 +255,19 @@
     table = jnp.where(used, table, 0.0)
 
     cmc_state, t_own = lax.optimization_barrier((cmc_state, t_own))
-    left_cells = jnp.concatenate([shift(cmc_state[:, :, -1:], "slab", 1), cmc_state[:, :, :-1]], axis=2)
-    right_cells = jnp.concatenate([cmc_state[:, :, 1:], shift(cmc_state[:, :, :1], "slab", -1)], axis=2)
-    moved = cmc_state - 0.4 * (cmc_state - left_cells) + 0.1 * (right_cells - 2.0 * cmc_state + left_cells)
-    moved = jnp.concatenate(
-        [shift(moved[:, -1:], "cross", 1), moved, shift(moved[:, :1], "cross", -1)], axis=1
-    )
+    moved = jnp.concatenate([bin_before, advect(cmc_state, left_end, right_end), bin_after], axis=1)
     moved = jnp.pad(moved.transpose(1, 0, 2), ((0, 0), (0, sp - species), (0, 0)))
 
-    blocks = [t_own]
+    blocks, wcs = [t_own], []
     bits = [1 << k for k in range(ncross.bit_length() - 1)][::-1]
+    acc, wc = bin_call(t_own, table, None, None, bins, cells, nshape)
+    wcs.append(wc)
     for bit in bits:
         got = swap(jnp.concatenate(blocks, axis=1) if len(blocks) > 1 else blocks[0], "cross", bit)
         if len(blocks) == 1:
-            got, moved = lax.optimization_barrier((got, moved))
+            got, moved, acc, wcs[0] = lax.optimization_barrier((got, moved, acc, wcs[0]))
         blocks.append(got)
-
-    acc, wcs = None, []
-    for block in blocks:
+    for block in blocks[1:]:
         acc, wc = bin_call(block, table, None, acc, bins, cells, nshape)
         wcs.append(wc)
     up = shift(acc[:, cells:], "slab", 1)
@@ -277,18 +293,28 @@
     from_below = shift(fresh, "slab", 1)
     from_above = shift(fresh, "slab", -1)
 
-    args = (own_bins, cells, nshape)
-    own_part = [project_call([fresh], (1,), b, w, None, *args) for b, w in zip(blocks, wcs)]
-    from_below, from_above, *own_part = lax.optimization_barrier((from_below, from_above, *own_part))
-    parts = [None] * len(blocks)
-    for n in reversed(range(len(blocks))):
-        parts[n] = project_call([from_below, from_above], (0, 2), blocks[n], wcs[n], own_part[n], *args)
-    for n, bit in reversed(list(enumerate(bits))):
-        got = swap(parts[n + 1], "cross", bit)
-        parts[0 : n + 1] = [
-            p + got[:, sum(q.shape[1] for q in parts[:k]) :][:, : p.shape[1]] for k, p in enumerate(parts[: n + 1])
-        ]
-    total = parts[0]
+    args = (count, own_bins, cells, nshape)
+    where = [(blocks[0], wcs[0], 0)]
+    for bit, block, wc in zip(bits, blocks[1:], wcs[1:]):
+        held = {r: n for n, r in enumerate(order)} if bit != bits[0] else {0: 0}
+        order = list(held) + [r ^ bit for r in held]
+        where += [(block, wc, n * count) for n in range(len(held))]
+    order = order if bits else [0]
+    places = dict(zip(order, where))
+    own_part = {r: project_call([fresh], (1,), *places[r][:2], None, places[r][2], *args) for r in order}
+    from_below, from_above, own_part = lax.optimization_barrier((from_below, from_above, own_part))
+
+    def reduced(who, bits, sides):
+        if not bits:
+            block, wc, place = places[who]
+            return project_call(sides, (0, 2), block, wc, own_part[who], place, *args)
+        far = reduced(who ^ bits[0], bits[1:], sides)
+        if len(bits) > 1:
+            far, sides = lax.optimization_barrier((far, sides))
+        got = swap(far, "cross", bits[0])
+        return reduced(who, bits[1:], sides) + got
+
+    total = reduced(0, bits, [from_below, from_above])
     conditional = (total[:species] / total[species : species + 1]).reshape(transported.shape)
     les_out = transported + 0.5 * (conditional - transported)
     return (les_out, cmc_out)

time: 265 us -> 263 us (level)
  local copies, waits for them, and re-layouts: 22.4 us -> 32.5 us
  waiting for transfers between devices: 24 us -> 14.6 us
  starting transfers between devices: 38.3 us -> 32.2 us
  other arithmetic: 11.1 us -> 14.5 us
    slice x5 -> x13, local copies, waits for them, and re-layouts: 5.19 us -> 11.2 us  [the longest x3 3.48 us: slab_end(): les_state[:, at].reshape(species, ends)]
    ppermute x4 -> x5, waiting for transfers between devices: 9.61 us -> 4.2 us  [swap(): return lax.ppermute(array, axis, [(i, i ^ bit) for i in range(count)])]
    ppermute x12 -> x8, starting transfers between devices: 30.6 us -> 25.4 us  [shift(): lax.ppermute(array, axis, [(i, i + by) for i in range(count) if 0 <= i +...]
    unnamed x54 -> x68, local copies, waits for them, and re-layouts: 4.4 us -> 9.06 us
    broadcast_in_dim x0 -> x6, local copies, waits for them, and re-layouts: none -> 4.01 us  [the longest x2 1.35 us: on_device(): from_right[:, ends:, None]]
    ppermute x12 -> x8, waiting for transfers between devices: 14.4 us -> 10.4 us  [shift(): lax.ppermute(array, axis, [(i, i + by) for i in range(count) if 0 <= i +...]
    concatenate x0 -> x4, other arithmetic: none -> 3.88 us  [the longest x2 2.45 us: slab_end(): jnp.concatenate([les_state[:, at].reshape(species, ends), cmc_state[:, :,...]
    optimization_barrier x2 -> x1, local copies, waits for them, and re-layouts: 3.45 us -> 0.52 us  [on_device(): cmc_state, t_own = lax.optimization_barrier((cmc_state, t_own))]
  transfers between devices with their start and end apart: 16 -> 13, of which waited for: 5 -> 3; matrix products, arithmetic and copies ran while one was open for 6% -> 7% of each run, Pallas kernels for 44% -> 48%
where the time goes in v3:
time: 263 us; the launch traced here: 262 us
  Pallas kernels  167 us (63%)
  local copies, waits for them, and re-layouts  32.5 us (12%)
  starting transfers between devices  32.2 us (12%)
  waiting for transfers between devices  14.6 us (6%)
  other arithmetic  14.5 us (6%)
    pallas_call x6, Pallas kernels, bin_call(): pl.pallas_call(functools.partial(bin_kernel, bins, sp, cells, nshape, out...  85.2 us
    pallas_call x8, Pallas kernels, project_call(): pl.pallas_call(functools.partial(project_kernel, bins, sp, cells, nshape,...  75.8 us
    ppermute x8, starting transfers between devices, shift(): lax.ppermute(array, axis, [(i, i + by) for i in range(count) if 0 <= i +...  25.4 us
    ppermute x8, waiting for transfers between devices, shift(): lax.ppermute(array, axis, [(i, i + by) for i in range(count) if 0 <= i +...  10.4 us
    unnamed x68, local copies, waits for them, and re-layouts  9.06 us
    ppermute x5, starting transfers between devices, swap(): return lax.ppermute(array, axis, [(i, i ^ bit) for i in range(count)])  6.87 us
    pallas_call x1, Pallas kernels, on_device(): pl.pallas_call(functools.partial(chem_kernel, species, sp), out_shape=jax...  5.97 us
  transfers between devices with their start and end apart: 13, of which 3 were waited for; matrix products, arithmetic and copies ran while one was open for 7% of the time, Pallas kernels for 48%

profile of v3, /device:TPU:0, one launch (start us, length us, event | category | flops | bytes accessed | tf_op | source)
XLA Modules:
  0.0 262.2 jit_solution(17591642494605567168)
XLA Ops:
  10.8 6.2 %collective-permute-start.1 = (f32[54,544]{0,1:T(8,128)}, f32[54,544]{0,1:T(8,128)}, u32[]{:S(2)}, u32[]{:S(2)}) collective-permute-start(f32[54,544]{0,1:T(8,128)} %pad_maximum_fusion.8), channel_id=1, source_target_pairs={{0,4},{4,8},{8,12},{12,16},{16,20},{20,24},{24,28},{1,5},{5,9},{9,... | collective-permute-start | bytes 352520 | tf_op jit(solution)/shard_map/ppermute | solution.py:19
  21.7 3.4 %collective-permute-done.1 = f32[54,544]{0,1:T(8,128)} collective-permute-done((f32[54,544]{0,1:T(8,128)}, f32[54,544]{0,1:T(8,128)}, u32[]{:S(2)}, u32[]{:S(2)}) %collective-permute-start.1) | collective-permute-done | bytes 117536 | tf_op jit(solution)/shard_map/ppermute | solution.py:19
  30.0 2.6 collective-permute-start.3
  46.6 4.0 %collective-permute-start.4 = (f32[56,4096]{1,0:T(8,128)S(1)}, f32[56,4096]{1,0:T(8,128)S(1)}, u32[]{:S(2)}, u32[]{:S(2)}) collective-permute-start(f32[56,4096]{1,0:T(8,128)S(1)} %pad_maximum_fusion.1.refs_0_.refs_1_.refs_2_), channel_id=1, source_target_pairs={{0,2},{1,3},{2,0},{3,1},{4,6},{5,7},{6,4},{7,5},{8,10},{9,11},{10,... | collective-permute-start | bytes 2752520 | tf_op jit(solution)/shard_map/ppermute | solution.py:24
  55.3 11.4 %bin_outer.3 = (f32[1904,256]{1,0:T(8,128)S(1)}, f32[40,4096]{1,0:T(8,128)S(1)}) custom-call(f32[56,4096]{1,0:T(8,128)S(1)} %pad_maximum_fusion.1.refs_0_.refs_1_.refs_2_, f32[40,128]{1,0:T(8,128)S(1)} %fusion.19.refs_1_), custom_call_target="tpu_custom_call" | custom-call | flops 499122176 | bytes 917504 | tf_op jit(solution)/shard_map/bin_outer/pallas_call | solution.py:107
  66.8 4.2 %collective-permute-done.4.refs_0_.refs_1_.refs_2_ = f32[56,4096]{1,0:T(8,128)S(1)} collective-permute-done((f32[56,4096]{1,0:T(8,128)S(1)}, f32[56,4096]{1,0:T(8,128)S(1)}, u32[]{:S(2)}, u32[]{:S(2)}) %collective-permute-start.4) | collective-permute-done | bytes 917536 | tf_op jit(solution)/shard_map/ppermute | solution.py:24
  71.9 11.4 %bin_outer.4 = (f32[1904,256]{1,0:T(8,128)S(1)}, f32[40,4096]{1,0:T(8,128)S(1)}) custom-call(f32[56,4096]{1,0:T(8,128)S(1)} %collective-permute-done.4.refs_0_.refs_1_.refs_2_, f32[40,128]{1,0:T(8,128)S(1)} %fusion.19.refs_1_, f32[1904,256]{1,0:T(8,128)S(1)} %get-tuple-element.31.refs_2_), custom_call_target="tpu_custom_call" | custom-call | flops 499122176 | bytes 917504 | tf_op jit(solution)/shard_map/bin_outer/pallas_call | solution.py:107
  84.2 22.6 %bin_outer.5 = (f32[1904,256]{1,0:T(8,128)S(1)}, f32[40,8192]{1,0:T(8,128)S(1)}) custom-call(f32[56,8192]{1,0:T(8,128)S(1)} %collective-permute-done.5.refs_0_.refs_1_.refs_2_, f32[40,128]{1,0:T(8,128)S(1)} %fusion.19.refs_1_, f32[1904,256]{1,0:T(8,128)S(1)} %get-tuple-element.32.refs_2_), custom_call_target="tpu_custom_call" | custom-call | flops 998244352 | bytes 1835008 | tf_op jit(solution)/shard_map/bin_outer/pallas_call | solution.py:107
  109.6 6.1 %collective-permute-start.6 = (f32[1904,128]{1,0:T(8,128)}, f32[1904,128]{1,0:T(8,128)}, u32[]{:S(2)}, u32[]{:S(2)}) collective-permute-start(f32[1904,128]{1,0:T(8,128)} %get-tuple-element.59), channel_id=1, source_target_pairs={{0,4},{4,8},{8,12},{12,16},{16,20},{20,24},{24,28},{1,5},{5,9},{9,... | collective-permute-start | bytes 2924552 | tf_op jit(solution)/shard_map/ppermute | solution.py:19
  119.6 9.9 %bin_own.3.refs_2_ = f32[1904,128]{1,0:T(8,128)S(1)} custom-call(f32[56,4096]{1,0:T(8,128)S(1)} %copy-done.1, f32[40,4096]{1,0:T(8,128)S(1)} %copy-done.6), custom_call_target="tpu_custom_call" | custom-call | flops 249561088 | bytes 917504 | tf_op jit(solution)/shard_map/bin_own/pallas_call | solution.py:107
  129.5 10.1 %bin_own.4.refs_2_ = f32[1904,128]{1,0:T(8,128)S(1)} custom-call(f32[56,4096]{1,0:T(8,128)S(1)} %copy-done.4, f32[40,4096]{1,0:T(8,128)S(1)} %copy-done.9, f32[1904,128]{1,0:T(8,128)S(1)} %bin_own.3.refs_2_), custom_call_target="tpu_custom_call" | custom-call | flops 249561088 | bytes 917504 | tf_op jit(solution)/shard_map/bin_own/pallas_call | solution.py:107
  139.7 19.7 %bin_own.5 = f32[1904,128]{1,0:T(8,128)S(1)} custom-call(f32[56,8192]{1,0:T(8,128)S(1)} %collective-permute-done.5.refs_0_.refs_1_.refs_2_, f32[40,8192]{1,0:T(8,128)S(1)} %get-tuple-element.37.refs_1_.refs_2_.refs_3_, f32[1904,128]{1,0:T(8,128)S(1)} %bin_own.4.refs_2_), custom_call_target="tpu_custom_call" | custom-call | flops 499122176 | bytes 1835008 | tf_op jit(solution)/shard_map/bin_own/pallas_call | solution.py:107
  159.5 6.0 %chem.1 = f32[32,56,128]{2,1,0:T(8,128)S(1)} custom-call(f32[34,56,128]{2,1,0:T(8,128)S(1)} %bitcast.57, f32[34,56,128]{2,1,0:T(8,128)} %bitcast.18.above_ref, f32[34,56,128]{2,1,0:T(8,128)} %bitcast.19.below_ref, f32[34,56,128]{2,1,0:T(8,128)S(1)} %copy-done.10, f32[32,128]{1,0:T(8,128)S(1)} %copy-done.11, f32[32,128]{1,0:T(8,128)S(1)} %copy-done.12, ...), custom_call_target="tpu_custom_call" | custom-call | tf_op jit(solution)/shard_map/chem/pallas_call | solution.py:282
  166.9 5.0 %collective-permute-start.8 = (f32[1792,128]{1,0:T(8,128)S(1)}, f32[1792,128]{1,0:T(8,128)S(1)}, u32[]{:S(2)}, u32[]{:S(2)}) collective-permute-start(f32[1792,128]{1,0:T(8,128)S(1)} %bitcast.52), channel_id=1, source_target_pairs={{0,4},{4,8},{8,12},{12,16},{16,20},{20,24},{24,28},{1,5},{5,9},{9,... | collective-permute-start | bytes 2752520 | tf_op jit(solution)/shard_map/ppermute | solution.py:19
  172.0 7.8 %project.10.refs_4_ = f32[56,4096]{1,0:T(8,128)S(1)} custom-call(f32[1792,128]{1,0:T(8,128)S(1)} %bitcast.53, f32[56,4096]{1,0:T(8,128)S(1)} %copy-done.4, f32[40,4096]{1,0:T(8,128)S(1)} %copy-done.9), custom_call_target="tpu_custom_call" | custom-call | flops 234881024 | bytes 1835008 | tf_op jit(solution)/shard_map/project/pallas_call | solution.py:193
  179.8 7.7 %project.8.refs_4_ = f32[56,4096]{1,0:T(8,128)S(1)} custom-call(f32[1792,128]{1,0:T(8,128)S(1)} %bitcast.54, f32[56,4096]{1,0:T(8,128)S(1)} %copy-done.2, f32[40,4096]{1,0:T(8,128)S(1)} %copy-done.7), custom_call_target="tpu_custom_call" | custom-call | flops 234881024 | bytes 1835008 | tf_op jit(solution)/shard_map/project/pallas_call | solution.py:193
  187.5 7.9 %project.11.refs_4_ = f32[56,4096]{1,0:T(8,128)S(1)} custom-call(f32[1792,128]{1,0:T(8,128)S(1)} %bitcast.55, f32[56,8192]{1,0:T(8,128)S(1)} %collective-permute-done.5.refs_0_.refs_1_.refs_2_, f32[40,8192]{1,0:T(8,128)S(1)} %get-tuple-element.37.refs_1_.refs_2_.refs_3_), custom_call_target="tpu_custom_call" | custom-call | flops 234881024 | bytes 1835008 | tf_op jit(solution)/shard_map/project/pallas_call | solution.py:193
  195.4 7.7 %project.9.refs_4_ = f32[56,4096]{1,0:T(8,128)S(1)} custom-call(f32[1792,128]{1,0:T(8,128)S(1)} %bitcast.56, f32[56,8192]{1,0:T(8,128)S(1)} %collective-permute-done.5.refs_0_.refs_1_.refs_2_, f32[40,8192]{1,0:T(8,128)S(1)} %get-tuple-element.37.refs_1_.refs_2_.refs_3_), custom_call_target="tpu_custom_call" | custom-call | flops 234881024 | bytes 1835008 | tf_op jit(solution)/shard_map/project/pallas_call | solution.py:193
  203.2 7.0 %collective-permute-done.8.refs_0_ = f32[1792,128]{1,0:T(8,128)S(1)} collective-permute-done((f32[1792,128]{1,0:T(8,128)S(1)}, f32[1792,128]{1,0:T(8,128)S(1)}, u32[]{:S(2)}, u32[]{:S(2)}) %collective-permute-start.8) | collective-permute-done | bytes 917536 | tf_op jit(solution)/shard_map/ppermute | solution.py:19
  210.2 11.3 %project.13 = f32[56,4096]{1,0:T(8,128)S(1)} custom-call(f32[1792,128]{1,0:T(8,128)S(1)} %collective-permute-done.8.refs_0_, f32[1792,128]{1,0:T(8,128)S(1)} %collective-permute-done.9.refs_1_, f32[56,8192]{1,0:T(8,128)S(1)} %collective-permute-done.5.refs_0_.refs_1_.refs_2_, f32[40,8192]{1,0:T(8,128)S(1)} %get-tuple-element.37.refs_1_.refs_2_.refs_3_, ...), custom_call_target="tpu_custom_call" | custom-call | flops 469762048 | bytes 1835008 | tf_op jit(solution)/shard_map/project/pallas_call | solution.py:193
  221.6 11.2 %project.12 = f32[56,4096]{1,0:T(8,128)S(1)} custom-call(f32[1792,128]{1,0:T(8,128)S(1)} %collective-permute-done.8.refs_0_, f32[1792,128]{1,0:T(8,128)S(1)} %collective-permute-done.9.refs_1_, f32[56,4096]{1,0:T(8,128)S(1)} %copy-done.4, f32[40,4096]{1,0:T(8,128)S(1)} %copy-done.9, f32[56,4096]{1,0:T(8,128)S(1)} %project.10.refs_4_), custom_call_target="tpu_custom_call" | custom-call | flops 469762048 | bytes 1835008 | tf_op jit(solution)/shard_map/project/pallas_call | solution.py:193
  234.5 11.1 %project.15 = f32[56,4096]{1,0:T(8,128)S(1)} custom-call(f32[1792,128]{1,0:T(8,128)S(1)} %collective-permute-done.8.refs_0_, f32[1792,128]{1,0:T(8,128)S(1)} %collective-permute-done.9.refs_1_, f32[56,8192]{1,0:T(8,128)S(1)} %collective-permute-done.5.refs_0_.refs_1_.refs_2_, f32[40,8192]{1,0:T(8,128)S(1)} %get-tuple-element.37.refs_1_.refs_2_.refs_3_, ...), custom_call_target="tpu_custom_call" | custom-call | flops 469762048 | bytes 1835008 | tf_op jit(solution)/shard_map/project/pallas_call | solution.py:193
  247.1 11.1 %project.14 = f32[56,4096]{1,0:T(8,128)S(1)} custom-call(f32[1792,128]{1,0:T(8,128)S(1)} %collective-permute-done.8.refs_0_, f32[1792,128]{1,0:T(8,128)S(1)} %collective-permute-done.9.refs_1_, f32[56,4096]{1,0:T(8,128)S(1)} %copy-done.2, f32[40,4096]{1,0:T(8,128)S(1)} %copy-done.7, f32[56,4096]{1,0:T(8,128)S(1)} %project.8.refs_4_), custom_call_target="tpu_custom_call" | custom-call | flops 469762048 | bytes 1835008 | tf_op jit(solution)/shard_map/project/pallas_call | solution.py:193
  259.7 2.5 multiply_add_fusion
  (137 shorter events, 52.7 us)
Async XLA Ops:
  4.9 13.1 %copy-start.15 = (f32[54,8,4,128]{3,2,1,0:T(4,128)S(1)}, f32[54,8,4,128]{3,2,1,0:T(4,128)}, u32[]{:S(2)}) copy-start(f32[54,8,4,128]{3,2,1,0:T(4,128)} %param.10) | copy-start | bytes 2654212
  5.5 12.4 %copy-start.24 = (s32[8,4,128]{2,1,0:T(4,128)S(1)}, s32[8,4,128]{2,1,0:T(4,128)}, u32[]{:S(2)}) copy-start(s32[8,4,128]{2,1,0:T(4,128)} %param.13) | copy-start | bytes 49156
  5.5 12.4 %copy-start.25 = (s32[8,4,128]{2,1,0:T(4,128)S(1)}, s32[8,4,128]{2,1,0:T(4,128)}, u32[]{:S(2)}) copy-start(s32[8,4,128]{2,1,0:T(4,128)} %param.12) | copy-start | bytes 49156
  5.5 13.6 %copy-start.22 = (f32[128,128]{1,0:T(8,128)S(1)}, f32[128,128]{1,0:T(8,128)}, u32[]{:S(2)}) copy-start(f32[128,128]{1,0:T(8,128)} %param.14) | copy-start | bytes 196612
  7.2 19.1 %collective-permute-start = (f32[54,544]{0,1:T(8,128)}, f32[54,544]{0,1:T(8,128)S(1)}, u32[]{:S(2)}, u32[]{:S(2)}) collective-permute-start(f32[54,544]{0,1:T(8,128)} %pad_maximum_fusion.7), channel_id=1, source_target_pairs={{4,0},{8,4},{12,8},{16,12},{20,16},{24,20},{28,24},{5,1},{9,5},{13... | collective-permute-start | bytes 352520 | tf_op jit(solution)/shard_map/ppermute | solution.py:19
  10.8 14.3 %collective-permute-start.1 = (f32[54,544]{0,1:T(8,128)}, f32[54,544]{0,1:T(8,128)}, u32[]{:S(2)}, u32[]{:S(2)}) collective-permute-start(f32[54,544]{0,1:T(8,128)} %pad_maximum_fusion.8), channel_id=1, source_target_pairs={{0,4},{4,8},{8,12},{12,16},{16,20},{20,24},{24,28},{1,5},{5,9},{9,... | collective-permute-start | bytes 352520 | tf_op jit(solution)/shard_map/ppermute | solution.py:19
  30.0 7.7 %collective-permute-start.3 = (f32[54,1152]{1,0:T(8,128)}, f32[54,1152]{1,0:T(8,128)}, u32[]{:S(2)}, u32[]{:S(2)}) collective-permute-start(f32[54,1152]{1,0:T(8,128)} %pad_maximum_fusion.10), channel_id=1, source_target_pairs={{0,1},{1,2},{2,3},{4,5},{5,6},{6,7},{8,9},{9,10},{10,11},{12,13},{... | collective-permute-start | bytes 746504 | tf_op jit(solution)/shard_map/ppermute | solution.py:19
  34.2 4.6 %collective-permute-start.2 = (f32[54,1152]{1,0:T(8,128)}, f32[54,1152]{1,0:T(8,128)}, u32[]{:S(2)}, u32[]{:S(2)}) collective-permute-start(f32[54,1152]{1,0:T(8,128)} %pad_maximum_fusion.9), channel_id=1, source_target_pairs={{1,0},{2,1},{3,2},{5,4},{6,5},{7,6},{9,8},{10,9},{11,10},{13,12},{... | collective-permute-start | bytes 746504 | tf_op jit(solution)/shard_map/ppermute | solution.py:19
  46.1 24.9 %copy-start = (f32[56,4096]{1,0:T(8,128)}, f32[56,4096]{1,0:T(8,128)S(1)}, u32[]{:S(2)}) copy-start(f32[56,4096]{1,0:T(8,128)S(1)} %pad_maximum_fusion.1.refs_0_.refs_1_.refs_2_) | copy-start | bytes 2752516
  46.6 24.4 %collective-permute-start.4 = (f32[56,4096]{1,0:T(8,128)S(1)}, f32[56,4096]{1,0:T(8,128)S(1)}, u32[]{:S(2)}, u32[]{:S(2)}) collective-permute-start(f32[56,4096]{1,0:T(8,128)S(1)} %pad_maximum_fusion.1.refs_0_.refs_1_.refs_2_), channel_id=1, source_target_pairs={{0,2},{1,3},{2,0},{3,1},{4,6},{5,7},{6,4},{7,5},{8,10},{9,11},{10,... | collective-permute-start | bytes 2752520 | tf_op jit(solution)/shard_map/ppermute | solution.py:24
  71.1 13.1 %collective-permute-start.5 = (f32[56,8192]{1,0:T(8,128)S(1)}, f32[56,8192]{1,0:T(8,128)S(1)}, u32[]{:S(2)}, u32[]{:S(2)}) collective-permute-start(f32[56,8192]{1,0:T(8,128)S(1)} %pad_maximum_fusion), channel_id=1, source_target_pairs={{0,1},{1,0},{2,3},{3,2},{4,5},{5,4},{6,7},{7,6},{8,9},{9,8},{10,11... | collective-permute-start | bytes 5505032 | tf_op jit(solution)/shard_map/ppermute | solution.py:24
  108.3 51.2 %collective-permute-start.7 = (f32[1904,128]{1,0:T(8,128)}, f32[1904,128]{1,0:T(8,128)}, u32[]{:S(2)}, u32[]{:S(2)}) collective-permute-start(f32[1904,128]{1,0:T(8,128)} %get-tuple-element.58), channel_id=1, source_target_pairs={{4,0},{8,4},{12,8},{16,12},{20,16},{24,20},{28,24},{5,1},{9,5},{13... | collective-permute-start | bytes 2924552 | tf_op jit(solution)/shard_map/ppermute | solution.py:19
  109.6 49.9 %collective-permute-start.6 = (f32[1904,128]{1,0:T(8,128)}, f32[1904,128]{1,0:T(8,128)}, u32[]{:S(2)}, u32[]{:S(2)}) collective-permute-start(f32[1904,128]{1,0:T(8,128)} %get-tuple-element.59), channel_id=1, source_target_pairs={{0,4},{4,8},{8,12},{12,16},{16,20},{20,24},{24,28},{1,5},{5,9},{9,... | collective-permute-start | bytes 2924552 | tf_op jit(solution)/shard_map/ppermute | solution.py:19
  139.7 19.8 %copy-start.10 = (f32[34,56,128]{2,1,0:T(8,128)S(1)}, f32[34,56,128]{2,1,0:T(8,128)}, u32[]{:S(2)}) copy-start(f32[34,56,128]{2,1,0:T(8,128)} %pad.17.moved_ref) | copy-start | bytes 2924548
  139.7 19.8 %copy-start.11 = (f32[32,128]{1,0:T(8,128)S(1)}, f32[32,128]{1,0:T(8,128)}, u32[]{:S(2)}) copy-start(f32[32,128]{1,0:T(8,128)} %diss_ref.1) | copy-start | bytes 49156
  139.7 19.8 %copy-start.12 = (f32[32,128]{1,0:T(8,128)S(1)}, f32[32,128]{1,0:T(8,128)}, u32[]{:S(2)}) copy-start(f32[32,128]{1,0:T(8,128)} %rate_ref.1) | copy-start | bytes 49156
  139.7 19.8 %copy-start.13 = (s32[128]{0:T(128)S(1)}, s32[128]{0:T(128)}, u32[]{:S(2)}) copy-start(s32[128]{0:T(128)} %param.19) | copy-start | bytes 1540
  165.5 14.3 %copy-start.2 = (f32[56,4096]{1,0:T(8,128)S(1)}, f32[56,4096]{1,0:T(8,128)}, u32[]{:S(2)}) copy-start(f32[56,4096]{1,0:T(8,128)} %copy-done) | copy-start | bytes 2752516
  165.5 14.3 %copy-start.7 = (f32[40,4096]{1,0:T(8,128)S(1)}, f32[40,4096]{1,0:T(8,128)}, u32[]{:S(2)}) copy-start(f32[40,4096]{1,0:T(8,128)} %copy-done.5) | copy-start | bytes 1966084
  165.5 37.7 %collective-permute-start.9 = (f32[1792,128]{1,0:T(8,128)S(1)}, f32[1792,128]{1,0:T(8,128)S(1)}, u32[]{:S(2)}, u32[]{:S(2)}) collective-permute-start(f32[1792,128]{1,0:T(8,128)S(1)} %bitcast.51), channel_id=1, source_target_pairs={{4,0},{8,4},{12,8},{16,12},{20,16},{24,20},{28,24},{5,1},{9,5},{13... | collective-permute-start | bytes 2752520 | tf_op jit(solution)/shard_map/ppermute | solution.py:19
  166.9 43.2 %collective-permute-start.8 = (f32[1792,128]{1,0:T(8,128)S(1)}, f32[1792,128]{1,0:T(8,128)S(1)}, u32[]{:S(2)}, u32[]{:S(2)}) collective-permute-start(f32[1792,128]{1,0:T(8,128)S(1)} %bitcast.52), channel_id=1, source_target_pairs={{0,4},{4,8},{8,12},{12,16},{16,20},{20,24},{24,28},{1,5},{5,9},{9,... | collective-permute-start | bytes 2752520 | tf_op jit(solution)/shard_map/ppermute | solution.py:19
  221.5 11.3 %collective-permute-start.10 = (f32[56,4096]{1,0:T(8,128)S(1)}, f32[56,4096]{1,0:T(8,128)S(1)}, u32[]{:S(2)}, u32[]{:S(2)}) collective-permute-start(f32[56,4096]{1,0:T(8,128)S(1)} %project.13), channel_id=1, source_target_pairs={{0,1},{1,0},{2,3},{3,2},{4,5},{5,4},{6,7},{7,6},{8,9},{9,8},{10,11... | collective-permute-start | bytes 2752520 | tf_op jit(solution)/shard_map/ppermute | solution.py:24
  232.8 25.4 %collective-permute-start.12 = (f32[56,4096]{1,0:T(8,128)S(1)}, f32[56,4096]{1,0:T(8,128)S(1)}, u32[]{:S(2)}, u32[]{:S(2)}) collective-permute-start(f32[56,4096]{1,0:T(8,128)S(1)} %add.86), channel_id=1, source_target_pairs={{0,2},{1,3},{2,0},{3,1},{4,6},{5,7},{6,4},{7,5},{8,10},{9,11},{10,... | collective-permute-start | bytes 2752520 | tf_op jit(solution)/shard_map/ppermute | solution.py:24
  245.7 12.6 %collective-permute-start.11 = (f32[56,4096]{1,0:T(8,128)S(1)}, f32[56,4096]{1,0:T(8,128)S(1)}, u32[]{:S(2)}, u32[]{:S(2)}) collective-permute-start(f32[56,4096]{1,0:T(8,128)S(1)} %project.15), channel_id=1, source_target_pairs={{0,1},{1,0},{2,3},{3,2},{4,5},{5,4},{6,7},{7,6},{8,9},{9,8},{10,11... | collective-permute-start | bytes 2752520 | tf_op jit(solution)/shard_map/ppermute | solution.py:24
  (16 other events, 66.7 us)

commit v4 on v3

--- a/solution.py
+++ b/solution.py
@@ -214,29 +214,10 @@
     count = cmc_map.size
     ncross = lax.axis_size("cross")
 
-    planes, ends = les_state.shape[1], les_state.shape[2] * les_state.shape[3]
-
-    def slab_end(at):
-        return jnp.concatenate([les_state[:, at].reshape(species, ends), cmc_state[:, :, at]], axis=1)
-
-    from_left, from_right = shift(slab_end(-1), "slab", 1), shift(slab_end(0), "slab", -1)
-    below, above = (g[:, :ends].reshape(les_state[:, :1].shape) for g in (from_left, from_right))
-    left_end, right_end = from_left[:, ends:, None], from_right[:, ends:, None]
-
-    def advect(state, left, right):
-        left = jnp.concatenate([left, state[:, :, :-1]], axis=2)
-        right = jnp.concatenate([state[:, :, 1:], right], axis=2)
-        return state - 0.4 * (state - left) + 0.1 * (right - 2.0 * state + left)
-
-    def cross_end(at):
-        rows = les_state[:, :, at].reshape(species, -1)
-        pick = slice(at, at + 1 or None)
-        bin_row = advect(cmc_state[:, pick], left_end[:, pick], right_end[:, pick])
-        return jnp.concatenate([rows, bin_row[:, 0]], axis=1)
-
-    from_behind, from_ahead = shift(cross_end(-1), "cross", 1), shift(cross_end(0), "cross", -1)
-    behind, ahead = (g[:, :-cells].reshape(les_state[:, :, :1].shape) for g in (from_behind, from_ahead))
-    bin_before, bin_after = from_behind[:, None, -cells:], from_ahead[:, None, -cells:]
+    below = shift(les_state[:, -1:], "slab", 1)
+    above = shift(les_state[:, :1], "slab", -1)
+    behind = shift(les_state[:, :, -1:], "cross", 1)
+    ahead = shift(les_state[:, :, :1], "cross", -1)
     xs = jnp.concatenate([below, les_state, above], axis=1)
     ys = jnp.concatenate([behind, les_state, ahead], axis=2)
     zs = jnp.pad(les_state, ((0, 0), (0, 0), (0, 0), (1, 1)))
@@ -255,19 +236,24 @@
     table = jnp.where(used, table, 0.0)
 
     cmc_state, t_own = lax.optimization_barrier((cmc_state, t_own))
-    moved = jnp.concatenate([bin_before, advect(cmc_state, left_end, right_end), bin_after], axis=1)
+    left_cells = jnp.concatenate([shift(cmc_state[:, :, -1:], "slab", 1), cmc_state[:, :, :-1]], axis=2)
+    right_cells = jnp.concatenate([cmc_state[:, :, 1:], shift(cmc_state[:, :, :1], "slab", -1)], axis=2)
+    moved = cmc_state - 0.4 * (cmc_state - left_cells) + 0.1 * (right_cells - 2.0 * cmc_state + left_cells)
+    moved = jnp.concatenate(
+        [shift(moved[:, -1:], "cross", 1), moved, shift(moved[:, :1], "cross", -1)], axis=1
+    )
     moved = jnp.pad(moved.transpose(1, 0, 2), ((0, 0), (0, sp - species), (0, 0)))
 
-    blocks, wcs = [t_own], []
+    blocks = [t_own]
     bits = [1 << k for k in range(ncross.bit_length() - 1)][::-1]
-    acc, wc = bin_call(t_own, table, None, None, bins, cells, nshape)
-    wcs.append(wc)
     for bit in bits:
         got = swap(jnp.concatenate(blocks, axis=1) if len(blocks) > 1 else blocks[0], "cross", bit)
         if len(blocks) == 1:
-            got, moved, acc, wcs[0] = lax.optimization_barrier((got, moved, acc, wcs[0]))
+            got, moved = lax.optimization_barrier((got, moved))
         blocks.append(got)
-    for block in blocks[1:]:
+
+    acc, wcs = None, []
+    for block in blocks:
         acc, wc = bin_call(block, table, None, acc, bins, cells, nshape)
         wcs.append(wc)
     up = shift(acc[:, cells:], "slab", 1)

time: 263 us -> 255 us (0.970)
  local copies, waits for them, and re-layouts: 32.5 us -> 22.4 us
  starting transfers between devices: 32.2 us -> 38.8 us
  other arithmetic: 14.5 us -> 10.4 us
    slice x13 -> x5, local copies, waits for them, and re-layouts: 11.2 us -> 5.29 us  [the longest x1 1.98 us: on_device(): ahead = shift(les_state[:, :, :1], 'cross', -1)]
    ppermute x8 -> x12, starting transfers between devices: 25.4 us -> 30.8 us  [shift(): lax.ppermute(array, axis, [(i, i + by) for i in range(count) if 0 <= i +...]
    ppermute x5, waiting for transfers between devices: 4.2 us -> 0.01 us  [swap(): return lax.ppermute(array, axis, [(i, i ^ bit) for i in range(count)])]
    broadcast_in_dim x6 -> x0, local copies, waits for them, and re-layouts: 4.01 us -> none  [the longest x2 1.35 us: on_device(): from_right[:, ends:, None]]
    concatenate x4 -> x0, other arithmetic: 3.88 us -> none  [the longest x2 2.45 us: slab_end(): jnp.concatenate([les_state[:, at].reshape(species, ends), cmc_state[:, :,...]
    ppermute x8 -> x12, waiting for transfers between devices: 10.4 us -> 14.1 us  [shift(): lax.ppermute(array, axis, [(i, i + by) for i in range(count) if 0 <= i +...]
    optimization_barrier x1 -> x2, local copies, waits for them, and re-layouts: 0.52 us -> 3.45 us  [on_device(): cmc_state, t_own = lax.optimization_barrier((cmc_state, t_own))]
    ppermute x0 -> x2, local copies, waits for them, and re-layouts: none -> 2.71 us  [shift(): lax.ppermute(array, axis, [(i, i + by) for i in range(count) if 0 <= i +...]
  transfers between devices with their start and end apart: 13 -> 17, of which waited for: 3 -> 4; matrix products, arithmetic and copies ran while one was open for 7% -> 5% of each run, Pallas kernels for 48% -> 50%
where the time goes in v4:
time: 255 us; the launch traced here: 254 us
  Pallas kernels  167 us (65%)
  starting transfers between devices  38.8 us (15%)
  local copies, waits for them, and re-layouts  22.4 us (9%)
  waiting for transfers between devices  14.1 us (6%)
  other arithmetic  10.4 us (4%)
    pallas_call x6, Pallas kernels, bin_call(): pl.pallas_call(functools.partial(bin_kernel, bins, sp, cells, nshape, out...  85.2 us
    pallas_call x8, Pallas kernels, project_call(): pl.pallas_call(functools.partial(project_kernel, bins, sp, cells, nshape,...  76 us
    ppermute x12, starting transfers between devices, shift(): lax.ppermute(array, axis, [(i, i + by) for i in range(count) if 0 <= i +...  30.8 us
    ppermute x12, waiting for transfers between devices, shift(): lax.ppermute(array, axis, [(i, i + by) for i in range(count) if 0 <= i +...  14.1 us
    ppermute x5, starting transfers between devices, swap(): return lax.ppermute(array, axis, [(i, i ^ bit) for i in range(count)])  8.04 us
    unnamed x58, local copies, waits for them, and re-layouts  7.32 us
    pallas_call x1, Pallas kernels, on_device(): pl.pallas_call(functools.partial(chem_kernel, species, sp), out_shape=jax...  5.97 us
  transfers between devices with their start and end apart: 17, of which 4 were waited for; matrix products, arithmetic and copies ran while one was open for 5% of the time, Pallas kernels for 50%

profile of v4, /device:TPU:0, one launch (start us, length us, event | category | flops | bytes accessed | tf_op | source)
XLA Modules:
  0.0 254.3 jit_solution(7995631748291764512)
XLA Ops:
  3.0 5.5 %collective-permute-start.1 = (f32[54,1,4,128]{3,2,1,0:T(4,128)S(1)}, f32[54,1,4,128]{3,2,1,0:T(4,128)S(1)}, u32[]{:S(2)}, u32[]{:S(2)}) collective-permute-start(f32[54,1,4,128]{3,2,1,0:T(4,128)S(1)} %get-tuple-element.61), channel_id=1, source_target_pairs={{0,4},{4,8},{8,12},{12,16},{16,20},{20,24},{24,28},{1,5},{5,9},{9,... | collective-permute-start | bytes 331784 | tf_op jit(solution)/shard_map/ppermute | solution.py:19
  14.1 3.3 %collective-permute-done.2 = f32[54,8,1,128]{3,1,2,0:T(8,128)S(1)} collective-permute-done((f32[54,8,1,128]{3,1,2,0:T(8,128)S(1)}, f32[54,8,1,128]{3,1,2,0:T(8,128)S(1)}, u32[]{:S(2)}, u32[]{:S(2)}) %collective-permute-start.2) | collective-permute-done | bytes 221216 | tf_op jit(solution)/shard_map/ppermute | solution.py:19
  21.5 2.9 %copy.34 = f32[54,32,128]{0,1,2:T(8,128)} copy(f32[54,32,128]{2,1,0:T(8,128)S(1)} %copy-done.15) | data formatting | bytes 1769472 | tf_op jit(solution)/shard_map/optimization_barrier | solution.py:238
  24.4 4.1 %collective-permute-start.4 = (f32[56,4096]{1,0:T(8,128)S(1)}, f32[56,4096]{1,0:T(8,128)S(1)}, u32[]{:S(2)}, u32[]{:S(2)}) collective-permute-start(f32[56,4096]{1,0:T(8,128)S(1)} %pad_maximum_fusion.1.refs_0_.refs_1_.refs_2_), channel_id=1, source_target_pairs={{0,2},{1,3},{2,0},{3,1},{4,6},{5,7},{6,4},{7,5},{8,10},{9,11},{10,... | collective-permute-start | bytes 2752520 | tf_op jit(solution)/shard_map/ppermute | solution.py:24
  29.3 4.3 %collective-permute-start.5 = (f32[54,32,1]{0,1,2:T(8,128)S(1)}, f32[54,32,1]{0,1,2:T(8,128)S(1)}, u32[]{:S(2)}, u32[]{:S(2)}) collective-permute-start(f32[54,32,1]{0,1,2:T(8,128)S(1)} %get-tuple-element.52), channel_id=1, source_target_pairs={{0,4},{4,8},{8,12},{12,16},{16,20},{20,24},{24,28},{1,5},{5,9},{9,... | collective-permute-start | bytes 20744 | tf_op jit(solution)/shard_map/ppermute | solution.py:19
  41.9 2.9 %fusion.2 = f32[54,32,128]{2,0,1:T(8,128)S(1)} fusion(f32[54,32,1]{2,0,1:T(8,128)} %copy.41, f32[54,32,127]{2,0,1:T(8,128)} %get-tuple-element.59, f32[54,32,127]{2,0,1:T(8,128)} %get-tuple-element.58, f32[54,32,1]{2,0,1:T(8,128)} %copy.36, f32[54,32,128]{2,1,0:T(8,128)S(1)} %copy-done.16), kind=kLoop, calls=%fused_computation.11 | loop fusion | flops 2211840 | bytes 3538944 | tf_op jit(solution)/shard_map/add | solution.py:241
  55.6 11.4 %bin_outer.3 = (f32[1904,256]{1,0:T(8,128)S(1)}, f32[40,4096]{1,0:T(8,128)S(1)}) custom-call(f32[56,4096]{1,0:T(8,128)S(1)} %pad_maximum_fusion.1.refs_0_.refs_1_.refs_2_, f32[40,128]{1,0:T(8,128)S(1)} %fusion.11.refs_1_), custom_call_target="tpu_custom_call" | custom-call | flops 499122176 | bytes 917504 | tf_op jit(solution)/shard_map/bin_outer/pallas_call | solution.py:107
  67.9 11.4 %bin_outer.4 = (f32[1904,256]{1,0:T(8,128)S(1)}, f32[40,4096]{1,0:T(8,128)S(1)}) custom-call(f32[56,4096]{1,0:T(8,128)S(1)} %copy-done.4, f32[40,128]{1,0:T(8,128)S(1)} %fusion.11.refs_1_, f32[1904,256]{1,0:T(8,128)S(1)} %get-tuple-element.27.refs_2_), custom_call_target="tpu_custom_call" | custom-call | flops 499122176 | bytes 917504 | tf_op jit(solution)/shard_map/bin_outer/pallas_call | solution.py:107
  80.1 22.7 %bin_outer.5 = (f32[1904,256]{1,0:T(8,128)S(1)}, f32[40,8192]{1,0:T(8,128)S(1)}) custom-call(f32[56,8192]{1,0:T(8,128)S(1)} %collective-permute-done.9.refs_0_.refs_1_.refs_2_, f32[40,128]{1,0:T(8,128)S(1)} %fusion.11.refs_1_, f32[1904,256]{1,0:T(8,128)S(1)} %get-tuple-element.28.refs_2_), custom_call_target="tpu_custom_call" | custom-call | flops 998244352 | bytes 1835008 | tf_op jit(solution)/shard_map/bin_outer/pallas_call | solution.py:107
  105.5 5.5 %collective-permute-start.10 = (f32[1904,128]{1,0:T(8,128)}, f32[1904,128]{1,0:T(8,128)}, u32[]{:S(2)}, u32[]{:S(2)}) collective-permute-start(f32[1904,128]{1,0:T(8,128)} %get-tuple-element.55), channel_id=1, source_target_pairs={{0,4},{4,8},{8,12},{12,16},{16,20},{20,24},{24,28},{1,5},{5,9},{9,... | collective-permute-start | bytes 2924552 | tf_op jit(solution)/shard_map/ppermute | solution.py:19
  113.5 9.9 %bin_own.3.refs_2_ = f32[1904,128]{1,0:T(8,128)S(1)} custom-call(f32[56,4096]{1,0:T(8,128)S(1)} %copy-done.1, f32[40,4096]{1,0:T(8,128)S(1)} %copy-done.7), custom_call_target="tpu_custom_call" | custom-call | flops 249561088 | bytes 917504 | tf_op jit(solution)/shard_map/bin_own/pallas_call | solution.py:107
  123.4 10.1 %bin_own.4.refs_2_ = f32[1904,128]{1,0:T(8,128)S(1)} custom-call(f32[56,4096]{1,0:T(8,128)S(1)} %copy-done.5, f32[40,4096]{1,0:T(8,128)S(1)} %copy-done.10, f32[1904,128]{1,0:T(8,128)S(1)} %bin_own.3.refs_2_), custom_call_target="tpu_custom_call" | custom-call | flops 249561088 | bytes 917504 | tf_op jit(solution)/shard_map/bin_own/pallas_call | solution.py:107
  133.6 19.7 %bin_own.5 = f32[1904,128]{1,0:T(8,128)S(1)} custom-call(f32[56,8192]{1,0:T(8,128)S(1)} %collective-permute-done.9.refs_0_.refs_1_.refs_2_, f32[40,8192]{1,0:T(8,128)S(1)} %get-tuple-element.33.refs_1_.refs_2_.refs_3_, f32[1904,128]{1,0:T(8,128)S(1)} %bin_own.4.refs_2_), custom_call_target="tpu_custom_call" | custom-call | flops 499122176 | bytes 1835008 | tf_op jit(solution)/shard_map/bin_own/pallas_call | solution.py:107
  153.4 6.0 %chem.1 = f32[32,56,128]{2,1,0:T(8,128)S(1)} custom-call(f32[34,56,128]{2,1,0:T(8,128)S(1)} %bitcast.23, f32[34,56,128]{2,1,0:T(8,128)} %bitcast.6.above_ref, f32[34,56,128]{2,1,0:T(8,128)} %bitcast.7.below_ref, f32[34,56,128]{2,1,0:T(8,128)S(1)} %copy-done.11, f32[32,128]{1,0:T(8,128)S(1)} %copy-done.12, f32[32,128]{1,0:T(8,128)S(1)} %copy-done.13, ...), custom_call_target="tpu_custom_call" | custom-call | tf_op jit(solution)/shard_map/chem/pallas_call | solution.py:268
  160.8 4.8 %collective-permute-start.12 = (f32[1792,128]{1,0:T(8,128)S(1)}, f32[1792,128]{1,0:T(8,128)S(1)}, u32[]{:S(2)}, u32[]{:S(2)}) collective-permute-start(f32[1792,128]{1,0:T(8,128)S(1)} %bitcast.18), channel_id=1, source_target_pairs={{0,4},{4,8},{8,12},{12,16},{16,20},{20,24},{24,28},{1,5},{5,9},{9,... | collective-permute-start | bytes 2752520 | tf_op jit(solution)/shard_map/ppermute | solution.py:19
  165.6 7.8 %project.10.refs_4_ = f32[56,4096]{1,0:T(8,128)S(1)} custom-call(f32[1792,128]{1,0:T(8,128)S(1)} %bitcast.19, f32[56,4096]{1,0:T(8,128)S(1)} %copy-done.5, f32[40,4096]{1,0:T(8,128)S(1)} %copy-done.10), custom_call_target="tpu_custom_call" | custom-call | flops 234881024 | bytes 1835008 | tf_op jit(solution)/shard_map/project/pallas_call | solution.py:193
  173.5 7.8 %project.8.refs_4_ = f32[56,4096]{1,0:T(8,128)S(1)} custom-call(f32[1792,128]{1,0:T(8,128)S(1)} %bitcast.20, f32[56,4096]{1,0:T(8,128)S(1)} %copy-done.2, f32[40,4096]{1,0:T(8,128)S(1)} %copy-done.8), custom_call_target="tpu_custom_call" | custom-call | flops 234881024 | bytes 1835008 | tf_op jit(solution)/shard_map/project/pallas_call | solution.py:193
  181.3 7.9 %project.11.refs_4_ = f32[56,4096]{1,0:T(8,128)S(1)} custom-call(f32[1792,128]{1,0:T(8,128)S(1)} %bitcast.21, f32[56,8192]{1,0:T(8,128)S(1)} %collective-permute-done.9.refs_0_.refs_1_.refs_2_, f32[40,8192]{1,0:T(8,128)S(1)} %get-tuple-element.33.refs_1_.refs_2_.refs_3_), custom_call_target="tpu_custom_call" | custom-call | flops 234881024 | bytes 1835008 | tf_op jit(solution)/shard_map/project/pallas_call | solution.py:193
  189.2 7.7 %project.9.refs_4_ = f32[56,4096]{1,0:T(8,128)S(1)} custom-call(f32[1792,128]{1,0:T(8,128)S(1)} %bitcast.22, f32[56,8192]{1,0:T(8,128)S(1)} %collective-permute-done.9.refs_0_.refs_1_.refs_2_, f32[40,8192]{1,0:T(8,128)S(1)} %get-tuple-element.33.refs_1_.refs_2_.refs_3_), custom_call_target="tpu_custom_call" | custom-call | flops 234881024 | bytes 1835008 | tf_op jit(solution)/shard_map/project/pallas_call | solution.py:193
  196.9 5.9 %collective-permute-done.12.refs_0_ = f32[1792,128]{1,0:T(8,128)S(1)} collective-permute-done((f32[1792,128]{1,0:T(8,128)S(1)}, f32[1792,128]{1,0:T(8,128)S(1)}, u32[]{:S(2)}, u32[]{:S(2)}) %collective-permute-start.12) | collective-permute-done | bytes 917536 | tf_op jit(solution)/shard_map/ppermute | solution.py:19
  202.9 11.3 %project.13 = f32[56,4096]{1,0:T(8,128)S(1)} custom-call(f32[1792,128]{1,0:T(8,128)S(1)} %collective-permute-done.12.refs_0_, f32[1792,128]{1,0:T(8,128)S(1)} %collective-permute-done.13.refs_1_, f32[56,8192]{1,0:T(8,128)S(1)} %collective-permute-done.9.refs_0_.refs_1_.refs_2_, f32[40,8192]{1,0:T(8,128)S(1)} %get-tuple-element.33.refs_1_.refs_2_.refs_3_, ...), custom_call_target="tpu_custom_call" | custom-call | flops 469762048 | bytes 1835008 | tf_op jit(solution)/shard_map/project/pallas_call | solution.py:193
  214.2 11.2 %project.12 = f32[56,4096]{1,0:T(8,128)S(1)} custom-call(f32[1792,128]{1,0:T(8,128)S(1)} %collective-permute-done.12.refs_0_, f32[1792,128]{1,0:T(8,128)S(1)} %collective-permute-done.13.refs_1_, f32[56,4096]{1,0:T(8,128)S(1)} %copy-done.5, f32[40,4096]{1,0:T(8,128)S(1)} %copy-done.10, f32[56,4096]{1,0:T(8,128)S(1)} %project.10.refs_4_), custom_call_target="tpu_custom_call" | custom-call | flops 469762048 | bytes 1835008 | tf_op jit(solution)/shard_map/project/pallas_call | solution.py:193
  226.5 11.1 %project.15 = f32[56,4096]{1,0:T(8,128)S(1)} custom-call(f32[1792,128]{1,0:T(8,128)S(1)} %collective-permute-done.12.refs_0_, f32[1792,128]{1,0:T(8,128)S(1)} %collective-permute-done.13.refs_1_, f32[56,8192]{1,0:T(8,128)S(1)} %collective-permute-done.9.refs_0_.refs_1_.refs_2_, f32[40,8192]{1,0:T(8,128)S(1)} %get-tuple-element.33.refs_1_.refs_2_.refs_3_, ...), custom_call_target="tpu_custom_call" | custom-call | flops 469762048 | bytes 1835008 | tf_op jit(solution)/shard_map/project/pallas_call | solution.py:193
  239.1 11.1 %project.14 = f32[56,4096]{1,0:T(8,128)S(1)} custom-call(f32[1792,128]{1,0:T(8,128)S(1)} %collective-permute-done.12.refs_0_, f32[1792,128]{1,0:T(8,128)S(1)} %collective-permute-done.13.refs_1_, f32[56,4096]{1,0:T(8,128)S(1)} %copy-done.2, f32[40,4096]{1,0:T(8,128)S(1)} %copy-done.8, f32[56,4096]{1,0:T(8,128)S(1)} %project.8.refs_4_), custom_call_target="tpu_custom_call" | custom-call | flops 469762048 | bytes 1835008 | tf_op jit(solution)/shard_map/project/pallas_call | solution.py:193
  (114 shorter events, 46.5 us)
Async XLA Ops:
  0.6 16.8 %copy-start.17 = (f32[54,8,4,128]{3,2,1,0:T(4,128)S(1)}, f32[54,8,4,128]{3,2,1,0:T(4,128)}, u32[]{:S(2)}) copy-start(f32[54,8,4,128]{3,2,1,0:T(4,128)} %param.10) | copy-start | bytes 2654212
  1.7 12.4 %collective-permute-start = (f32[54,1,4,128]{3,2,1,0:T(4,128)S(1)}, f32[54,1,4,128]{3,2,1,0:T(4,128)S(1)}, u32[]{:S(2)}, u32[]{:S(2)}) collective-permute-start(f32[54,1,4,128]{3,2,1,0:T(4,128)S(1)} %get-tuple-element.60), channel_id=1, source_target_pairs={{4,0},{8,4},{12,8},{16,12},{20,16},{24,20},{28,24},{5,1},{9,5},{13... | collective-permute-start | bytes 331784 | tf_op jit(solution)/shard_map/ppermute | solution.py:19
  3.0 11.1 %collective-permute-start.1 = (f32[54,1,4,128]{3,2,1,0:T(4,128)S(1)}, f32[54,1,4,128]{3,2,1,0:T(4,128)S(1)}, u32[]{:S(2)}, u32[]{:S(2)}) collective-permute-start(f32[54,1,4,128]{3,2,1,0:T(4,128)S(1)} %get-tuple-element.61), channel_id=1, source_target_pairs={{0,4},{4,8},{8,12},{12,16},{16,20},{20,24},{24,28},{1,5},{5,9},{9,... | collective-permute-start | bytes 331784 | tf_op jit(solution)/shard_map/ppermute | solution.py:19
  10.5 3.6 %collective-permute-start.3 = (f32[54,8,1,128]{3,1,2,0:T(8,128)S(1)}, f32[54,8,1,128]{3,1,2,0:T(8,128)S(1)}, u32[]{:S(2)}, u32[]{:S(2)}) collective-permute-start(f32[54,8,1,128]{3,1,2,0:T(8,128)S(1)} %bitcast.31), channel_id=1, source_target_pairs={{0,1},{1,2},{2,3},{4,5},{5,6},{6,7},{8,9},{9,10},{10,11},{12,13},{... | collective-permute-start | bytes 663560 | tf_op jit(solution)/shard_map/ppermute | solution.py:19
  12.0 5.5 %collective-permute-start.2 = (f32[54,8,1,128]{3,1,2,0:T(8,128)S(1)}, f32[54,8,1,128]{3,1,2,0:T(8,128)S(1)}, u32[]{:S(2)}, u32[]{:S(2)}) collective-permute-start(f32[54,8,1,128]{3,1,2,0:T(8,128)S(1)} %bitcast.30), channel_id=1, source_target_pairs={{1,0},{2,1},{3,2},{5,4},{6,5},{7,6},{9,8},{10,9},{11,10},{13,12},{... | collective-permute-start | bytes 663560 | tf_op jit(solution)/shard_map/ppermute | solution.py:19
  21.0 34.7 %copy-start = (f32[56,4096]{1,0:T(8,128)}, f32[56,4096]{1,0:T(8,128)S(1)}, u32[]{:S(2)}) copy-start(f32[56,4096]{1,0:T(8,128)S(1)} %pad_maximum_fusion.1.refs_0_.refs_1_.refs_2_) | copy-start | bytes 2752516
  24.4 26.1 %collective-permute-start.4 = (f32[56,4096]{1,0:T(8,128)S(1)}, f32[56,4096]{1,0:T(8,128)S(1)}, u32[]{:S(2)}, u32[]{:S(2)}) collective-permute-start(f32[56,4096]{1,0:T(8,128)S(1)} %pad_maximum_fusion.1.refs_0_.refs_1_.refs_2_), channel_id=1, source_target_pairs={{0,2},{1,3},{2,0},{3,1},{4,6},{5,7},{6,4},{7,5},{8,10},{9,11},{10,... | collective-permute-start | bytes 2752520 | tf_op jit(solution)/shard_map/ppermute | solution.py:24
  29.3 11.3 %collective-permute-start.5 = (f32[54,32,1]{0,1,2:T(8,128)S(1)}, f32[54,32,1]{0,1,2:T(8,128)S(1)}, u32[]{:S(2)}, u32[]{:S(2)}) collective-permute-start(f32[54,32,1]{0,1,2:T(8,128)S(1)} %get-tuple-element.52), channel_id=1, source_target_pairs={{0,4},{4,8},{8,12},{12,16},{16,20},{20,24},{24,28},{1,5},{5,9},{9,... | collective-permute-start | bytes 20744 | tf_op jit(solution)/shard_map/ppermute | solution.py:19
  33.5 5.6 %collective-permute-start.6 = (f32[54,32,1]{0,1,2:T(8,128)S(1)}, f32[54,32,1]{0,1,2:T(8,128)S(1)}, u32[]{:S(2)}, u32[]{:S(2)}) collective-permute-start(f32[54,32,1]{0,1,2:T(8,128)S(1)} %get-tuple-element.53), channel_id=1, source_target_pairs={{4,0},{8,4},{12,8},{16,12},{20,16},{24,20},{28,24},{5,1},{9,5},{13... | collective-permute-start | bytes 20744 | tf_op jit(solution)/shard_map/ppermute | solution.py:19
  44.8 2.6 %collective-permute-start.7 = (f32[54,1,128]{2,0,1:T(8,128)S(1)}, f32[54,1,128]{2,0,1:T(8,128)S(1)}, u32[]{:S(2)}, u32[]{:S(2)}) collective-permute-start(f32[54,1,128]{2,0,1:T(8,128)S(1)} %get-tuple-element.56), channel_id=1, source_target_pairs={{0,1},{1,2},{2,3},{4,5},{5,6},{6,7},{8,9},{9,10},{10,11},{12,13},{... | collective-permute-start | bytes 82952 | tf_op jit(solution)/shard_map/ppermute | solution.py:19
  46.1 3.3 %collective-permute-start.8 = (f32[54,1,128]{2,0,1:T(8,128)S(1)}, f32[54,1,128]{2,0,1:T(8,128)S(1)}, u32[]{:S(2)}, u32[]{:S(2)}) collective-permute-start(f32[54,1,128]{2,0,1:T(8,128)S(1)} %get-tuple-element.57), channel_id=1, source_target_pairs={{1,0},{2,1},{3,2},{5,4},{6,5},{7,6},{9,8},{10,9},{11,10},{13,12},{... | collective-permute-start | bytes 82952 | tf_op jit(solution)/shard_map/ppermute | solution.py:19
  52.8 27.3 %collective-permute-start.9 = (f32[56,8192]{1,0:T(8,128)}, f32[56,8192]{1,0:T(8,128)S(1)}, u32[]{:S(2)}, u32[]{:S(2)}) collective-permute-start(f32[56,8192]{1,0:T(8,128)} %pad_maximum_fusion), channel_id=1, source_target_pairs={{0,1},{1,0},{2,3},{3,2},{4,5},{5,4},{6,7},{7,6},{8,9},{9,8},{10,11... | collective-permute-start | bytes 5505032 | tf_op jit(solution)/shard_map/ppermute | solution.py:24
  104.2 49.1 %collective-permute-start.11 = (f32[1904,128]{1,0:T(8,128)}, f32[1904,128]{1,0:T(8,128)}, u32[]{:S(2)}, u32[]{:S(2)}) collective-permute-start(f32[1904,128]{1,0:T(8,128)} %get-tuple-element.54), channel_id=1, source_target_pairs={{4,0},{8,4},{12,8},{16,12},{20,16},{24,20},{28,24},{5,1},{9,5},{13... | collective-permute-start | bytes 2924552 | tf_op jit(solution)/shard_map/ppermute | solution.py:19
  105.5 47.8 %collective-permute-start.10 = (f32[1904,128]{1,0:T(8,128)}, f32[1904,128]{1,0:T(8,128)}, u32[]{:S(2)}, u32[]{:S(2)}) collective-permute-start(f32[1904,128]{1,0:T(8,128)} %get-tuple-element.55), channel_id=1, source_target_pairs={{0,4},{4,8},{8,12},{12,16},{16,20},{20,24},{24,28},{1,5},{5,9},{9,... | collective-permute-start | bytes 2924552 | tf_op jit(solution)/shard_map/ppermute | solution.py:19
  133.5 19.8 %copy-start.11 = (f32[34,56,128]{2,1,0:T(8,128)S(1)}, f32[34,56,128]{2,1,0:T(8,128)}, u32[]{:S(2)}) copy-start(f32[34,56,128]{2,1,0:T(8,128)} %pad.17.moved_ref) | copy-start | bytes 2924548
  133.5 19.8 %copy-start.12 = (f32[32,128]{1,0:T(8,128)S(1)}, f32[32,128]{1,0:T(8,128)}, u32[]{:S(2)}) copy-start(f32[32,128]{1,0:T(8,128)} %diss_ref.1) | copy-start | bytes 49156
  133.6 19.8 %copy-start.13 = (f32[32,128]{1,0:T(8,128)S(1)}, f32[32,128]{1,0:T(8,128)}, u32[]{:S(2)}) copy-start(f32[32,128]{1,0:T(8,128)} %rate_ref.1) | copy-start | bytes 49156
  133.6 19.8 %copy-start.14 = (s32[128]{0:T(128)S(1)}, s32[128]{0:T(128)}, u32[]{:S(2)}) copy-start(s32[128]{0:T(128)} %param.19) | copy-start | bytes 1540
  159.3 14.1 %copy-start.2 = (f32[56,4096]{1,0:T(8,128)S(1)}, f32[56,4096]{1,0:T(8,128)}, u32[]{:S(2)}) copy-start(f32[56,4096]{1,0:T(8,128)} %copy-done) | copy-start | bytes 2752516
  159.4 37.6 %collective-permute-start.13 = (f32[1792,128]{1,0:T(8,128)S(1)}, f32[1792,128]{1,0:T(8,128)S(1)}, u32[]{:S(2)}, u32[]{:S(2)}) collective-permute-start(f32[1792,128]{1,0:T(8,128)S(1)} %bitcast.17), channel_id=1, source_target_pairs={{4,0},{8,4},{12,8},{16,12},{20,16},{24,20},{28,24},{5,1},{9,5},{13... | collective-permute-start | bytes 2752520 | tf_op jit(solution)/shard_map/ppermute | solution.py:19
  160.8 42.1 %collective-permute-start.12 = (f32[1792,128]{1,0:T(8,128)S(1)}, f32[1792,128]{1,0:T(8,128)S(1)}, u32[]{:S(2)}, u32[]{:S(2)}) collective-permute-start(f32[1792,128]{1,0:T(8,128)S(1)} %bitcast.18), channel_id=1, source_target_pairs={{0,4},{4,8},{8,12},{12,16},{16,20},{20,24},{24,28},{1,5},{5,9},{9,... | collective-permute-start | bytes 2752520 | tf_op jit(solution)/shard_map/ppermute | solution.py:19
  214.1 11.3 %collective-permute-start.14 = (f32[56,4096]{1,0:T(8,128)S(1)}, f32[56,4096]{1,0:T(8,128)S(1)}, u32[]{:S(2)}, u32[]{:S(2)}) collective-permute-start(f32[56,4096]{1,0:T(8,128)S(1)} %project.13), channel_id=1, source_target_pairs={{0,1},{1,0},{2,3},{3,2},{4,5},{5,4},{6,7},{7,6},{8,9},{9,8},{10,11... | collective-permute-start | bytes 2752520 | tf_op jit(solution)/shard_map/ppermute | solution.py:24
  225.6 24.7 %collective-permute-start.16 = (f32[56,4096]{1,0:T(8,128)S(1)}, f32[56,4096]{1,0:T(8,128)S(1)}, u32[]{:S(2)}, u32[]{:S(2)}) collective-permute-start(f32[56,4096]{1,0:T(8,128)S(1)} %add.70), channel_id=1, source_target_pairs={{0,2},{1,3},{2,0},{3,1},{4,6},{5,7},{6,4},{7,5},{8,10},{9,11},{10,... | collective-permute-start | bytes 2752520 | tf_op jit(solution)/shard_map/ppermute | solution.py:24
  237.7 12.6 %collective-permute-start.15 = (f32[56,4096]{1,0:T(8,128)S(1)}, f32[56,4096]{1,0:T(8,128)S(1)}, u32[]{:S(2)}, u32[]{:S(2)}) collective-permute-start(f32[56,4096]{1,0:T(8,128)S(1)} %project.15), channel_id=1, source_target_pairs={{0,1},{1,0},{2,3},{3,2},{4,5},{5,4},{6,7},{7,6},{8,9},{9,8},{10,11... | collective-permute-start | bytes 2752520 | tf_op jit(solution)/shard_map/ppermute | solution.py:24
  (21 other events, 92.1 us)
